TPU v7x, 128 devices: a whole 4x4x4 slice. The times are simulated.
128 devices in a mesh: dom: 16 (over y, z), dir: 8 (over x, core).
Axes of the slice: x: 4, y: 4, z: 4, core: 2. Of those that a mesh axis runs over, the one named last changes fastest.
Arguments:
- unknowns: bfloat16 [512, 8, 1024], P(('dom', 'dir')), may hold values from -6 to 6
- schur_blocks: bfloat16 [512, 1024, 1024], P(('dom', 'dir')), may hold values from -0.1875 to 0.1875
- adjacency: int32 [512, 4], P(('dom', 'dir')), may hold values from 0 to 511, as said below
- row_map: int32 [512, 4, 1024], P(('dom', 'dir')), may hold values from 0 to 1023
- coupling: float32 [512, 4, 1024], P(('dom', 'dir')), may hold values from -1.5 to 1.5
- owner_box: int32 [512, 256, 1], P(('dom', 'dir')), may hold values from 0 to 1023; in each aligned block of 1024 rows (0 to 1023, 1024 to 2047, ..., all dimensions but the last counted through in order) at most 2 rows name the same one
- aggregation: bfloat16 [1024, 256, 1152], P('dom', None, 'dir'), may hold values from -0.1875 to 0.1875
- trans_table: float32 [316, 1152], P(None, 'dir'), may hold values from -1.5 to 1.5
- inter_list: int32 [1024, 16], P('dom'), may hold values from 0 to 1023, as said below
- inter_type: int32 [1024, 16], P('dom'), may hold values from 0 to 315
- near_list: int32 [1024, 4], P(('dom', 'dir')), may hold values from 0 to 63
- near_blocks: bfloat16 [1024, 4, 256, 256], P(('dom', 'dir')), may hold values from -0.375 to 0.375
Outputs:
- response: float32 [512, 8, 1024], P(('dom', 'dir'))
Inputs may be any that keep to these rules, and one draw needn't show every extreme that they name: `adjacency`: every neighbour t of subdomain s has t // 32 equal to g - 1, g or g + 1 modulo 16, with g = s // 32, and (t // 4) % 8 = (s // 4) % 8. `owner_box`: among the surface unknowns of one aligned block of 4 subdomains, no box is named more than 2 times. `inter_list`: every source box c of box b has c // 64 equal to b // 64 - 1, b // 64 or b // 64 + 1 modulo 16.
All inputs are finite; a program needn't handle non-finite values.
Results may differ from a plain program's by a relative error of at most 0.0035.
Values may be sent and summed in bfloat16 or wider, within the bound.
No kernel may reach another device: no remote copies, remote signals or barrier semaphores. Data moves between devices by JAX's collectives and lax.ppermute only.
A program may use at most 128 MiB of HBM per device.

v0:
```python
import functools

import jax
import jax.numpy as jnp
from jax import lax
from jax.experimental import pallas as pl
from jax.experimental.pallas import tpu as pltpu
from jax.sharding import PartitionSpec as P

F32 = jnp.float32
BF16 = jnp.bfloat16
I32 = jnp.int32
LANES = 128


def lane_pick(source, index):
    return jnp.take_along_axis(source, index, axis=1, mode="promise_in_bounds")


def iota(shape, axis):
    return lax.broadcasted_iota(I32, shape, axis)


def whole(shape):
    return pl.BlockSpec(shape, lambda *_: (0,) * len(shape))


SMEM_SPEC = pl.BlockSpec(memory_space=pltpu.SMEM)
ANY_SPEC = pl.BlockSpec(memory_space=pl.ANY)


def place_kernel(surface_ref, owner_ref, out_ref, spot_ref):
    blocks = owner_ref.shape[0]
    groups, copies = out_ref.shape[:2]
    box_tiles = groups // 2
    far_off = float(blocks * LANES)
    owner = owner_ref[...]
    lane = iota((LANES, LANES), 1).astype(F32)
    row = iota((LANES, LANES), 0).astype(F32)
    lowest = [None] * box_tiles
    total = [None] * box_tiles
    for t in range(blocks):
        spread = jnp.broadcast_to(owner[t : t + 1, :].astype(F32), (LANES, LANES))
        column = jnp.transpose(spread)
        number = row + (t * LANES - far_off)
        for b in range(box_tiles):
            hit = jnp.where(column == lane + float(b * LANES), number, 0.0)
            hit = hit.reshape(LANES // 8, 8, LANES)
            low = jnp.min(hit, axis=0)
            add = jnp.sum(hit, axis=0)
            lowest[b] = low if t == 0 else jnp.minimum(lowest[b], low)
            total[b] = add if t == 0 else total[b] + add
    lane8 = iota((8, LANES), 1)
    firsts = []
    seconds = []
    for b in range(box_tiles):
        low = jnp.min(lowest[b], axis=0, keepdims=True)
        add = jnp.sum(total[b], axis=0, keepdims=True)
        firsts.append(jnp.broadcast_to((low + far_off).astype(I32), (8, LANES)))
        seconds.append(jnp.broadcast_to((add - low + far_off).astype(I32), (8, LANES)))
    pieces = []
    for t in range(blocks):
        half = (t % 2) * LANES
        pieces.append(surface_ref[t // 2, :, half : half + LANES].astype(F32))
    for g in range(groups):
        b = g // 2
        if g % 2 == 0:
            source = jnp.where(lane8 < 64, firsts[b], pltpu.roll(seconds[b], 64, 1))
        else:
            source = jnp.where(lane8 < 64, pltpu.roll(firsts[b], 64, 1), seconds[b])
        within = source & (LANES - 1)
        block = source >> 7
        value = jnp.zeros((8, LANES), F32)
        for t in range(blocks):
            value = jnp.where(block == t, lane_pick(pieces[t], within), value)
        value = value.astype(BF16)
        for r in range(copies):
            out_ref[g, r] = value
    within = owner & (LANES - 1)
    box_tile = owner >> 7
    first = jnp.zeros((8, LANES), I32)
    for b in range(box_tiles):
        first = jnp.where(box_tile == b, lane_pick(firsts[b], within), first)
    own_number = iota((8, LANES), 0) * LANES + lane8
    rank = jnp.where(first == own_number, 0, 1)
    spot_ref[...] = (owner >> 6) * LANES + rank * 64 + (owner & 63)


def place(unknowns, owners, groups, copies):
    subs, excitations, _ = unknowns.shape
    surface = owners.size // subs
    return pl.pallas_call(
        place_kernel,
        grid=(1,),
        in_specs=[whole((subs, excitations, surface)), whole(owners.shape)],
        out_specs=[whole((groups, copies, excitations, LANES)), whole(owners.shape)],
        out_shape=[
            jax.ShapeDtypeStruct((groups, copies, excitations, LANES), BF16),
            jax.ShapeDtypeStruct(owners.shape, I32),
        ],
        cost_estimate=pl.CostEstimate(
            flops=8 * 1024 * 1024, bytes_accessed=300_000, transcendentals=0
        ),
        name="place",
    )(unknowns, owners)


def slot_order(count_dom, count_dir, transposed):
    size = 2 * count_dom * count_dir
    arrival = iota((size, size), 1 if transposed else 0)
    slot = iota((size, size), 0 if transposed else 1)
    source = arrival & (LANES - 1)
    shift = count_dir.bit_length() - 1
    target = ((source & (count_dir - 1)) * count_dom + (source >> shift)) * 2 + (arrival >> 7)
    return jnp.where(target == slot, 1.0, 0.0).astype(BF16)


def radiate_kernel(counts, arrived_ref, agg_ref, pattern_ref, current_ref, wide, turned):
    step = pl.program_id(0)
    boxes = pattern_ref.shape[0]
    excitations = arrived_ref.shape[1]
    half = arrived_ref.shape[2] // 2

    @pl.when(step == 0)
    def _():
        wide[...] = arrived_ref[...].astype(F32)
        for e in range(excitations):
            turned[:, e, :] = jnp.transpose(wide[:, e, :])
        first = turned[0:half].reshape(half * excitations, LANES)
        second = turned[half : 2 * half].reshape(half * excitations, LANES)
        both = jnp.concatenate([first, second], axis=1).astype(BF16)
        ordered = jnp.dot(both, slot_order(*counts, False), preferred_element_type=F32)
        current_ref[...] = ordered.astype(BF16).reshape(half, excitations, 2 * LANES)

    for n in range(boxes):
        field = lax.dot_general(
            current_ref[step * boxes + n],
            agg_ref[n],
            (((1,), (1,)), ((), ())),
            preferred_element_type=F32,
        )
        pattern_ref[n] = field.astype(BF16)


def radiate(arrived, agg, counts, step_boxes=8):
    sources, excitations, width = arrived.shape
    boxes, directions, slots = agg.shape
    return pl.pallas_call(
        functools.partial(radiate_kernel, counts),
        grid=(boxes // step_boxes,),
        in_specs=[
            whole(arrived.shape),
            pl.BlockSpec((step_boxes, directions, slots), lambda i: (i, 0, 0)),
        ],
        out_specs=[
            pl.BlockSpec((step_boxes, excitations, directions), lambda i: (i, 0, 0)),
            whole((boxes, excitations, slots)),
        ],
        out_shape=[
            jax.ShapeDtypeStruct((boxes, excitations, directions), BF16),
            jax.ShapeDtypeStruct((boxes, excitations, slots), BF16),
        ],
        scratch_shapes=[
            pltpu.VMEM((sources, excitations, width), F32),
            pltpu.VMEM((width, excitations, sources), F32),
        ],
        cost_estimate=pl.CostEstimate(
            flops=2 * boxes * 8 * directions * slots,
            bytes_accessed=2 * boxes * directions * slots,
            transcendentals=0,
        ),
        name="radiate",
    )(arrived, agg)


def near_kernel(near_ref, current_ref, block_ref, out_ref):
    step = pl.program_id(0)
    count = block_ref.shape[1]
    total = None
    for j in range(count):
        field = lax.dot_general(
            current_ref[near_ref[step * count + j]],
            block_ref[0, j],
            (((1,), (1,)), ((), ())),
            preferred_element_type=F32,
        )
        total = field if j == 0 else total + field
    out_ref[0] = total


def near(near_list, current, blocks):
    own, count, slots, _ = blocks.shape
    excitations = current.shape[1]
    return pl.pallas_call(
        near_kernel,
        grid=(own,),
        in_specs=[
            SMEM_SPEC,
            whole(current.shape),
            pl.BlockSpec((1, count, slots, slots), lambda i: (i, 0, 0, 0)),
        ],
        out_specs=pl.BlockSpec((1, excitations, slots), lambda i: (i, 0, 0)),
        out_shape=jax.ShapeDtypeStruct((own, excitations, slots), F32),
        cost_estimate=pl.CostEstimate(
            flops=2 * own * count * 8 * slots * slots,
            bytes_accessed=2 * own * count * slots * slots,
            transcendentals=0,
        ),
        name="near",
    )(near_list, current, blocks)


def couple_kernel(source_ref, before_ref, here_ref, after_ref, map_ref, coupling_ref,
                  schur_ref, out_ref, window):
    subs, links, width = map_ref.shape
    tiles = width // LANES
    window[0:subs] = before_ref[...].astype(F32)
    window[subs : 2 * subs] = here_ref[...].astype(F32)
    window[2 * subs : 3 * subs] = after_ref[...].astype(F32)
    out_ref[...] = schur_ref[...]

    def subdomain(s, carry):
        for k in range(links):
            base = source_ref[s * links + k]
            pieces = [window[base, :, q * LANES : (q + 1) * LANES] for q in range(tiles)]
            for t in range(tiles):
                cut = slice(t * LANES, (t + 1) * LANES)
                rows = jnp.broadcast_to(map_ref[s, k : k + 1, cut], (8, LANES))
                scale = jnp.broadcast_to(coupling_ref[s, k : k + 1, cut], (8, LANES))
                within = rows & (LANES - 1)
                tile = rows >> 7
                value = lane_pick(pieces[0], within)
                for q in range(1, tiles):
                    value = jnp.where(tile == q, lane_pick(pieces[q], within), value)
                out_ref[s, :, cut] += scale * value
        return carry

    lax.fori_loop(0, subs, subdomain, 0)


def couple(sources, before, here, after, row_map, coupling, schur):
    subs, excitations, width = here.shape
    same = whole(here.shape)
    return pl.pallas_call(
        couple_kernel,
        grid=(1,),
        in_specs=[SMEM_SPEC, same, same, same, whole(row_map.shape), whole(coupling.shape), same],
        out_specs=same,
        out_shape=jax.ShapeDtypeStruct(here.shape, F32),
        scratch_shapes=[pltpu.VMEM((3 * subs, excitations, width), F32)],
        cost_estimate=pl.CostEstimate(
            flops=8 * 1024 * 1024, bytes_accessed=8_000_000, transcendentals=0
        ),
        name="couple",
    )(sources, before, here, after, row_map, coupling, schur)


def receive_kernel(counts, place_ref, kind_ref, own_ref, before_ref, here_ref, after_ref,
                   table_ref, agg_ref, near_ref, out_ref, nearby, result, turned):
    step = pl.program_id(0)
    boxes, directions, slots = agg_ref.shape
    group = here_ref.shape[0]
    excitations = here_ref.shape[1]
    length = place_ref.shape[0] // group
    tail = directions - LANES

    @pl.when(step == 0)
    def _():
        nearby[0:group] = before_ref[...].astype(F32)
        nearby[group : 2 * group] = here_ref[...].astype(F32)
        nearby[2 * group : 3 * group] = after_ref[...].astype(F32)

    mine = (own_ref[0] == step).astype(F32)
    for n in range(boxes):
        head_sum = jnp.zeros((excitations, LANES), F32)
        tail_sum = jnp.zeros((excitations, tail), F32)
        for j in range(length):
            entry = (step * boxes + n) * length + j
            spot = place_ref[entry]
            kind = kind_ref[entry]
            factor = table_ref[pl.ds(kind, 1), :]
            head_sum += nearby[spot, :, 0:LANES] * factor[:, 0:LANES]
            tail_sum += nearby[spot, :, LANES:directions] * factor[:, LANES:directions]
        incoming = jnp.concatenate([head_sum, tail_sum], axis=1).astype(BF16)
        field = jnp.dot(incoming, agg_ref[n], preferred_element_type=F32)
        field = field + mine * near_ref[n]
        result[step * boxes + n] = field.astype(BF16)

    @pl.when(step == pl.num_programs(0) - 1)
    def _():
        flat = result[...].reshape(group * excitations, slots)
        ordered = jnp.dot(flat, slot_order(*counts, True), preferred_element_type=F32)
        nearby[0:group, :, 0:LANES] = ordered[:, 0:LANES].reshape(group, excitations, LANES)
        nearby[group : 2 * group, :, 0:LANES] = ordered[:, LANES:].reshape(
            group, excitations, LANES
        )
        for e in range(excitations):
            turned[:, e, :] = jnp.transpose(nearby[0 : 2 * group, e, 0:LANES])
        out_ref[...] = turned[...].astype(BF16)


def receive(places, kinds, own, before, here, after, table, agg, near_part, counts, step_boxes=8):
    boxes, directions, slots = agg.shape
    excitations = here.shape[1]
    targets = slots // 2
    same = whole(here.shape)
    return pl.pallas_call(
        functools.partial(receive_kernel, counts),
        grid=(boxes // step_boxes,),
        in_specs=[
            SMEM_SPEC,
            SMEM_SPEC,
            SMEM_SPEC,
            same,
            same,
            same,
            whole(table.shape),
            pl.BlockSpec((step_boxes, directions, slots), lambda i: (i, 0, 0)),
            whole(near_part.shape),
        ],
        out_specs=whole((targets, excitations, 2 * boxes)),
        out_shape=jax.ShapeDtypeStruct((targets, excitations, 2 * boxes), BF16),
        scratch_shapes=[
            pltpu.VMEM((3 * boxes, excitations, directions), F32),
            pltpu.VMEM((boxes, excitations, slots), BF16),
            pltpu.VMEM((targets, excitations, 2 * boxes), F32),
        ],
        cost_estimate=pl.CostEstimate(
            flops=2 * boxes * 8 * directions * slots,
            bytes_accessed=4 * boxes * directions * slots,
            transcendentals=0,
        ),
        name="receive",
    )(places, kinds, own, before, here, after, table, agg, near_part)


def finish_kernel(copies, term_ref, spot_ref, base_ref, out_ref):
    groups = term_ref.shape[0] // copies
    fields = []
    for g in range(groups):
        total = term_ref[g * copies].astype(F32)
        for k in range(1, copies):
            total = total + term_ref[g * copies + k].astype(F32)
        fields.append(total.astype(BF16).astype(F32))
    out_ref[...] = base_ref[...]
    for t in range(spot_ref.shape[0]):
        spot = jnp.broadcast_to(spot_ref[t : t + 1, :], (8, LANES))
        within = spot & (LANES - 1)
        group = spot >> 7
        value = lane_pick(fields[0], within)
        for g in range(1, groups):
            value = jnp.where(group == g, lane_pick(fields[g], within), value)
        half = (t % 2) * LANES
        out_ref[t // 2, :, half : half + LANES] += value


def finish(terms, spots, base, copies):
    return pl.pallas_call(
        functools.partial(finish_kernel, copies),
        grid=(1,),
        in_specs=[whole(terms.shape), whole(spots.shape), whole(base.shape)],
        out_specs=whole(base.shape),
        out_shape=jax.ShapeDtypeStruct(base.shape, F32),
        cost_estimate=pl.CostEstimate(
            flops=8 * 1024 * 128, bytes_accessed=600_000, transcendentals=0
        ),
        name="finish",
    )(terms, spots, base)


def both_ways(value, axis):
    count = lax.axis_size(axis)
    up = [(i, (i + 1) % count) for i in range(count)]
    down = [(j, i) for i, j in up]
    return lax.ppermute(value, axis, up), lax.ppermute(value, axis, down)


def exchange(value):
    return lax.all_to_all(value, ("dom", "dir"), split_axis=0, concat_axis=0, tiled=True)


def shards(unknowns, schur_blocks, adjacency, row_map, coupling, owner_box, aggregation,
           trans_table, inter_list, inter_type, near_list, near_blocks):
    doms = lax.axis_size("dom")
    dirs = lax.axis_size("dir")
    dom_here = lax.axis_index("dom")
    dir_here = lax.axis_index("dir")
    counts = (doms, dirs)
    subs, excitations, _ = unknowns.shape
    group = aggregation.shape[0]
    agg = jnp.swapaxes(aggregation, 1, 2)

    owners = owner_box.reshape(-1, LANES)
    placed, spots = place(unknowns, owners, doms, dirs)
    arrived = exchange(placed.reshape(doms * dirs, excitations, 2 * group))

    before_u, after_u = both_ways(unknowns, "dom")
    schur_part = jnp.einsum(
        "sij,sej->sei", schur_blocks, unknowns, preferred_element_type=F32
    )
    source_dom = adjacency // (subs * dirs)
    links = ((source_dom - dom_here + 1 + doms) % doms) * subs + adjacency % subs
    places = ((inter_list // group - dom_here + 1 + doms) % doms) * group + inter_list % group

    patterns, current = radiate(arrived, agg, counts)
    before_p, after_p = both_ways(patterns, "dom")
    near_part = near(near_list.reshape(-1), current, near_blocks)
    base = couple(links.reshape(-1), before_u, unknowns, after_u, row_map, coupling, schur_part)
    terms = receive(places.reshape(-1), inter_type.reshape(-1), dir_here.reshape(1), before_p,
                    patterns, after_p, trans_table, agg, near_part, counts)
    gathered = exchange(terms)
    return finish(gathered, spots, base, dirs)


def solution(mesh):
    split = ("dom", "dir")
    in_specs = (
        P(split, None, None),
        P(split, None, None),
        P(split, None),
        P(split, None, None),
        P(split, None, None),
        P(split, None, None),
        P("dom", None, "dir"),
        P(None, "dir"),
        P("dom", None),
        P("dom", None),
        P(split, None),
        P(split, None, None, None),
    )
    out_specs = P(split, None, None)
    return jax.shard_map(shards, mesh=mesh, in_specs=in_specs, out_specs=out_specs, check_vma=False)
```

profile of v0, /device:TPU:1, one launch (start us, length us, event | category | flops | bytes accessed | tf_op | source)
XLA Modules:
  0.0 78.2 jit_solution(10463061207379589946)
XLA Ops:
  0.0 2.7 %place.1 = (bf16[16,8,8,128]{3,2,1,0:T(8,128)(2,1)}, s32[8,128]{1,0:T(8,128)}) custom-call(bf16[4,8,1024]{2,1,0:T(8,128)(2,1)} %here_ref.1, s32[8,128]{1,0:T(8,128)} %bitcast.9), custom_call_target="tpu_custom_call" | custom-call | flops 8388608 | bytes 300000 | tf_op jit(solution)/shard_map/place/pallas_call | solution.py:92
  2.7 11.5 %all-to-all-start = ((bf16[128,8,128]{2,1,0:T(8,128)(2,1)}), bf16[128,8,128]{2,1,0:T(8,128)(2,1)S(1)}, u32[]{:S(2)}, u32[]{:S(2)}) async-start(bf16[128,8,128]{2,1,0:T(8,128)(2,1)} %bitcast.8), calls=%async_computation | async-start | bytes 524288 | tf_op jit(solution)/shard_map/all_to_all | solution.py:379
  14.2 1.6 %collective-permute-start.2 = (bf16[4,8,1024]{2,1,0:T(8,128)(2,1)}, bf16[4,8,1024]{2,1,0:T(8,128)(2,1)S(1)}, u32[]{:S(2)}, u32[]{:S(2)}) collective-permute-start(bf16[4,8,1024]{2,1,0:T(8,128)(2,1)} %here_ref.1), channel_id=1, source_target_pairs={{0,8},{8,16},{16,24},{24,32},{32,40},{40,48},{48,56},{56,64},{64,7... | collective-permute-start | bytes 196616 | tf_op jit(solution)/shard_map/ppermute | solution.py:375
  15.8 4.1 %collective-permute-start.3 = (bf16[4,8,1024]{2,1,0:T(8,128)(2,1)}, bf16[4,8,1024]{2,1,0:T(8,128)(2,1)S(1)}, u32[]{:S(2)}, u32[]{:S(2)}) collective-permute-start(bf16[4,8,1024]{2,1,0:T(8,128)(2,1)} %here_ref.1), channel_id=1, source_target_pairs={{8,0},{16,8},{24,16},{32,24},{40,32},{48,40},{56,48},{64,56},{72,6... | collective-permute-start | bytes 196616 | tf_op jit(solution)/shard_map/ppermute | solution.py:375
  19.9 0.8 copy.17
  20.7 0.7 reshape.26.near_ref
  21.3 3.9 %all-to-all-done.arrived_ref = bf16[128,8,128]{2,1,0:T(8,128)(2,1)S(1)} async-done(((bf16[128,8,128]{2,1,0:T(8,128)(2,1)}), bf16[128,8,128]{2,1,0:T(8,128)(2,1)S(1)}, u32[]{:S(2)}, u32[]{:S(2)}) %all-to-all-start) | async-done | bytes 262176 | tf_op jit(solution)/shard_map/all_to_all | solution.py:379
  25.2 0.0 copy-start
  25.2 0.7 copy-done
  25.9 0.0 copy-start.2
  25.9 7.6 %radiate.1 = (bf16[64,8,144]{2,1,0:T(8,128)(2,1)}, bf16[64,8,256]{2,1,0:T(8,128)(2,1)}) custom-call(bf16[128,8,128]{2,1,0:T(8,128)(2,1)} %copy-done, bf16[64,144,256]{2,1,0:T(8,128)(2,1)} %bitcast.6), custom_call_target="tpu_custom_call" | custom-call | flops 37748736 | bytes 4718592 | tf_op jit(solution)/shard_map/radiate/pallas_call | solution.py:148
  33.5 0.4 collective-permute-start
  33.9 4.4 %collective-permute-start.1 = (bf16[64,8,144]{2,1,0:T(8,128)(2,1)}, bf16[64,8,144]{2,1,0:T(8,128)(2,1)S(1)}, u32[]{:S(2)}, u32[]{:S(2)}) collective-permute-start(bf16[64,8,144]{2,1,0:T(8,128)(2,1)} %get-tuple-element.10.here_ref), channel_id=1, source_target_pairs={{8,0},{16,8},{24,16},{32,24},{40,32},{48,40},{56,48},{64,56},{72,6... | collective-permute-start | bytes 442376 | tf_op jit(solution)/shard_map/ppermute | solution.py:375
  38.3 0.7 fusion.4
  39.0 0.1 copy.15
  39.1 0.7 reshape.21.place_ref
  39.8 1.8 %copy.18.table_ref = f32[316,144]{1,0:T(8,128)} copy(f32[316,144]{0,1:T(8,128)} %param.19) | data formatting | bytes 364032 | tf_op args[7]
  41.6 0.8 copy.16
  42.4 0.7 reshape.22.kind_ref
  43.1 6.6 %near.1.near_ref = f32[8,8,256]{2,1,0:T(8,128)} custom-call(s32[32]{0:T(128)} %reshape.26.near_ref, bf16[64,8,256]{2,1,0:T(8,128)(2,1)} %get-tuple-element.11.current_ref, bf16[8,4,256,256]{3,2,1,0:T(8,128)(2,1)} %block_ref.1), custom_call_target="tpu_custom_call" | custom-call | flops 33554432 | bytes 4194304 | tf_op jit(solution)/shard_map/near/pallas_call | solution.py:194
  49.6 0.0 copy-start.7
  49.6 0.0 collective-permute-done.before_ref
  49.7 0.0 copy-start.3
  49.7 0.0 collective-permute-done.1.after_ref
  49.7 0.0 copy-start.4
  49.7 0.7 copy-done.3
  50.3 0.1 copy-done.4
  50.5 8.6 %receive.1 = bf16[128,8,128]{2,1,0:T(8,128)(2,1)} custom-call(s32[1024]{0:T(1024)} %reshape.21.place_ref, s32[1024]{0:T(1024)} %reshape.22.kind_ref, s32[1]{0:T(128)} %bitcast.own_ref, bf16[64,8,144]{2,1,0:T(8,128)(2,1)} %copy-done.3, bf16[64,8,144]{2,1,0:T(8,128)(2,1)} %get-tuple-element.10.here_ref, bf16[64,8,144]{2,1,0:T(8,128)(2,1)} %copy-done.4, ...), custom_call_target="tpu_custom_call" | custom-call | flops 37748736 | bytes 9437184 | tf_op jit(solution)/shard_map/receive/pallas_call | solution.py:307
  59.1 4.7 %all-to-all-start.1 = ((bf16[128,8,128]{2,1,0:T(8,128)(2,1)}), bf16[128,8,128]{2,1,0:T(8,128)(2,1)S(1)}, u32[]{:S(2)}, u32[]{:S(2)}) async-start(bf16[128,8,128]{2,1,0:T(8,128)(2,1)} %receive.1), calls=%async_computation.1 | async-start | bytes 524288 | tf_op jit(solution)/shard_map/all_to_all | solution.py:379
  63.8 0.0 copy-done.2
  63.8 6.3 %fusion.13.schur_ref = f32[4,8,1024]{2,1,0:T(8,128)} fusion(bf16[4,8,1024]{2,1,0:T(8,128)(2,1)S(1)} %copy-done.2, bf16[4,1024,1024]{2,1,0:T(8,128)(2,1)} %param.13), kind=kOutput, calls=%fused_computation.32 | convolution fusion | flops 67108864 | bytes 8585216 | tf_op jit(solution)/shard_map/sij,sej->sei/dot_general | solution.py:398
  70.1 0.0 copy-done.7
  70.1 0.7 reshape.27.source_ref
  70.8 0.0 collective-permute-done.2.before_ref
  70.8 0.0 copy-start.5
  70.8 0.0 collective-permute-done.3.after_ref
  70.8 0.6 copy-done.5
  71.4 0.0 copy-start.6
  71.4 0.6 copy-done.6
  72.1 3.6 %couple.1.base_ref = f32[4,8,1024]{2,1,0:T(8,128)} custom-call(s32[16]{0:T(128)} %reshape.27.source_ref, bf16[4,8,1024]{2,1,0:T(8,128)(2,1)} %copy-done.5, bf16[4,8,1024]{2,1,0:T(8,128)(2,1)} %here_ref.1, bf16[4,8,1024]{2,1,0:T(8,128)(2,1)} %copy-done.6, s32[4,4,1024]{2,1,0:T(4,128)} %map_ref.1, f32[4,4,1024]{2,1,0:T(4,128)} %coupling_ref.1, ...), custom_call_target="tpu_custom_call" | custom-call | flops 8388608 | bytes 8000000 | tf_op jit(solution)/shard_map/couple/pallas_call | solution.py:244
  75.7 0.0 all-to-all-done.1.term_ref
  75.7 0.0 copy-start.1
  75.7 0.7 copy-done.1
  76.4 1.8 %finish.1 = f32[4,8,1024]{2,1,0:T(8,128)} custom-call(bf16[128,8,128]{2,1,0:T(8,128)(2,1)} %copy-done.1, s32[8,128]{1,0:T(8,128)} %get-tuple-element.12.spot_ref, f32[4,8,1024]{2,1,0:T(8,128)} %couple.1.base_ref), custom_call_target="tpu_custom_call" | custom-call | flops 1048576 | bytes 600000 | tf_op jit(solution)/shard_map/finish/pallas_call | solution.py:358
  (1 shorter events, 0.0 us)
Async XLA Ops:
  2.7 22.5 %all-to-all-start = ((bf16[128,8,128]{2,1,0:T(8,128)(2,1)}), bf16[128,8,128]{2,1,0:T(8,128)(2,1)S(1)}, u32[]{:S(2)}, u32[]{:S(2)}) async-start(bf16[128,8,128]{2,1,0:T(8,128)(2,1)} %bitcast.8), calls=%async_computation | async-start | bytes 524288 | tf_op jit(solution)/shard_map/all_to_all | solution.py:379
  14.2 56.6 %collective-permute-start.2 = (bf16[4,8,1024]{2,1,0:T(8,128)(2,1)}, bf16[4,8,1024]{2,1,0:T(8,128)(2,1)S(1)}, u32[]{:S(2)}, u32[]{:S(2)}) collective-permute-start(bf16[4,8,1024]{2,1,0:T(8,128)(2,1)} %here_ref.1), channel_id=1, source_target_pairs={{0,8},{8,16},{16,24},{24,32},{32,40},{40,48},{48,56},{56,64},{64,7... | collective-permute-start | bytes 196616 | tf_op jit(solution)/shard_map/ppermute | solution.py:375
  15.8 55.0 %collective-permute-start.3 = (bf16[4,8,1024]{2,1,0:T(8,128)(2,1)}, bf16[4,8,1024]{2,1,0:T(8,128)(2,1)S(1)}, u32[]{:S(2)}, u32[]{:S(2)}) collective-permute-start(bf16[4,8,1024]{2,1,0:T(8,128)(2,1)} %here_ref.1), channel_id=1, source_target_pairs={{8,0},{16,8},{24,16},{32,24},{40,32},{48,40},{56,48},{64,56},{72,6... | collective-permute-start | bytes 196616 | tf_op jit(solution)/shard_map/ppermute | solution.py:375
  25.2 0.7 copy-start
  25.9 37.9 %copy-start.2 = (bf16[4,8,1024]{2,1,0:T(8,128)(2,1)S(1)}, bf16[4,8,1024]{2,1,0:T(8,128)(2,1)}, u32[]{:S(2)}) copy-start(bf16[4,8,1024]{2,1,0:T(8,128)(2,1)} %here_ref.1) | copy-start | bytes 196612
  33.5 16.1 %collective-permute-start = (bf16[64,8,144]{2,1,0:T(8,128)(2,1)}, bf16[64,8,144]{2,1,0:T(8,128)(2,1)S(1)}, u32[]{:S(2)}, u32[]{:S(2)}) collective-permute-start(bf16[64,8,144]{2,1,0:T(8,128)(2,1)} %get-tuple-element.10.here_ref), channel_id=1, source_target_pairs={{0,8},{8,16},{16,24},{24,32},{32,40},{40,48},{48,56},{56,64},{64,7... | collective-permute-start | bytes 442376 | tf_op jit(solution)/shard_map/ppermute | solution.py:375
  33.9 15.7 %collective-permute-start.1 = (bf16[64,8,144]{2,1,0:T(8,128)(2,1)}, bf16[64,8,144]{2,1,0:T(8,128)(2,1)S(1)}, u32[]{:S(2)}, u32[]{:S(2)}) collective-permute-start(bf16[64,8,144]{2,1,0:T(8,128)(2,1)} %get-tuple-element.10.here_ref), channel_id=1, source_target_pairs={{8,0},{16,8},{24,16},{32,24},{40,32},{48,40},{56,48},{64,56},{72,6... | collective-permute-start | bytes 442376 | tf_op jit(solution)/shard_map/ppermute | solution.py:375
  49.6 20.5 %copy-start.7 = (s32[4,4]{1,0:T(4,128)S(1)}, s32[4,4]{1,0:T(4,128)}, u32[]{:S(2)}) copy-start(s32[4,4]{1,0:T(4,128)} %param.14) | copy-start | bytes 196
  49.7 0.7 copy-start.3
  49.7 0.8 %copy-start.4 = (bf16[64,8,144]{2,1,0:T(8,128)(2,1)}, bf16[64,8,144]{2,1,0:T(8,128)(2,1)S(1)}, u32[]{:S(2)}) copy-start(bf16[64,8,144]{2,1,0:T(8,128)(2,1)S(1)} %collective-permute-done.1.after_ref) | copy-start | bytes 442372
  59.1 16.6 %all-to-all-start.1 = ((bf16[128,8,128]{2,1,0:T(8,128)(2,1)}), bf16[128,8,128]{2,1,0:T(8,128)(2,1)S(1)}, u32[]{:S(2)}, u32[]{:S(2)}) async-start(bf16[128,8,128]{2,1,0:T(8,128)(2,1)} %receive.1), calls=%async_computation.1 | async-start | bytes 524288 | tf_op jit(solution)/shard_map/all_to_all | solution.py:379
  70.8 0.6 copy-start.5
  71.4 0.6 copy-start.6
  75.7 0.7 copy-start.1
where the time goes:
time: 79.1 us; the launch traced here: 78.2 us
  Pallas kernels  31 us (39%)
  starting transfers between devices  26.7 us (34%)
  local copies, waits for them, and re-layouts  9.51 us (12%)
  matrix products  6.31 us (8%)
  waiting for transfers between devices  3.93 us (5%)
    all_to_all x2, starting transfers between devices, exchange(): lax.all_to_all(value, ('dom', 'dir'), split_axis=0, concat_axis=0, tiled=...  16.2 us
    ppermute x4, starting transfers between devices, both_ways(): return (lax.ppermute(value, axis, up), lax.ppermute(value, axis, down))  10.5 us
    pallas_call x1, Pallas kernels, receive(): pl.pallas_call(functools.partial(receive_kernel, counts), grid=(boxes //...  8.62 us
    pallas_call x1, Pallas kernels, radiate(): pl.pallas_call(functools.partial(radiate_kernel, counts), grid=(boxes //...  7.6 us
    unnamed x19, local copies, waits for them, and re-layouts  6.75 us
    pallas_call x1, Pallas kernels, near(): pl.pallas_call(near_kernel, grid=(own,), in_specs=[SMEM_SPEC, whole(curre...  6.59 us
    dot_general x1, matrix products, shards(): jnp.einsum('sij,sej->sei', schur_blocks, unknowns, preferred_element_type...  6.31 us
    all_to_all x2, waiting for transfers between devices, exchange(): lax.all_to_all(value, ('dom', 'dir'), split_axis=0, concat_axis=0, tiled=...  3.92 us
  transfers between devices with their start and end apart: 6, of which 1 were waited for; matrix products, arithmetic and copies ran while one was open for 17% of the time, Pallas kernels for 34%

commit v1 on v0

v1 whole, which is shorter than its diff:
```python
import functools

import jax
import jax.numpy as jnp
from jax import lax
from jax.experimental import pallas as pl
from jax.experimental.pallas import tpu as pltpu
from jax.sharding import PartitionSpec as P

F32 = jnp.float32
BF16 = jnp.bfloat16
I32 = jnp.int32
LANES = 128


def lane_pick(source, index):
    return jnp.take_along_axis(source, index, axis=1, mode="promise_in_bounds")


def iota(shape, axis):
    return lax.broadcasted_iota(I32, shape, axis)


SMEM_SPEC = pl.BlockSpec(memory_space=pltpu.SMEM)
VMEM_SPEC = pl.BlockSpec(memory_space=pltpu.VMEM)
HBM_SPEC = pl.BlockSpec(memory_space=pltpu.HBM)
VMEM_BYTES = 67_043_328
MIB = 1024 * 1024


def on_chip(kernel, name, spaces, operands, outputs, scratch=(), flops=0, moved=0, room=12 * MIB):
    specs = [{"s": SMEM_SPEC, "v": VMEM_SPEC, "h": HBM_SPEC}[c] for c in spaces]
    count = len(operands)
    several = isinstance(outputs, list)
    return pl.pallas_call(
        kernel,
        in_specs=specs[:count],
        out_specs=specs[count:] if several else specs[count],
        out_shape=outputs,
        scratch_shapes=list(scratch),
        compiler_params=pltpu.CompilerParams(vmem_limit_bytes=VMEM_BYTES - room),
        cost_estimate=pl.CostEstimate(flops=flops, bytes_accessed=moved, transcendentals=0),
        name=name,
    )(*operands)


def place_kernel(unknown_hbm, owner_hbm, out_hbm, spot_ref, surface_ref, owner_ref, value_ref,
                 arrive, leave):
    blocks = owner_ref.shape[0]
    groups, copies = out_hbm.shape[:2]
    owner_copy = pltpu.make_async_copy(owner_hbm, owner_ref, arrive.at[0])
    surface_copy = pltpu.make_async_copy(
        unknown_hbm.at[:, :, pl.ds(0, surface_ref.shape[2])], surface_ref, arrive.at[1]
    )
    owner_copy.start()
    surface_copy.start()
    owner_copy.wait()
    box_tiles = groups // 2
    far_off = float(blocks * LANES)
    owner = owner_ref[...]
    lane = iota((LANES, LANES), 1).astype(F32)
    row = iota((LANES, LANES), 0).astype(F32)
    lowest = [None] * box_tiles
    total = [None] * box_tiles
    for t in range(blocks):
        spread = jnp.broadcast_to(owner[t : t + 1, :].astype(F32), (LANES, LANES))
        column = jnp.transpose(spread)
        number = row + (t * LANES - far_off)
        for b in range(box_tiles):
            hit = jnp.where(column == lane + float(b * LANES), number, 0.0)
            hit = hit.reshape(LANES // 8, 8, LANES)
            low = jnp.min(hit, axis=0)
            add = jnp.sum(hit, axis=0)
            lowest[b] = low if t == 0 else jnp.minimum(lowest[b], low)
            total[b] = add if t == 0 else total[b] + add
    lane8 = iota((8, LANES), 1)
    firsts = []
    seconds = []
    for b in range(box_tiles):
        low = jnp.min(lowest[b], axis=0, keepdims=True)
        add = jnp.sum(total[b], axis=0, keepdims=True)
        firsts.append(jnp.broadcast_to((low + far_off).astype(I32), (8, LANES)))
        seconds.append(jnp.broadcast_to((add - low + far_off).astype(I32), (8, LANES)))
    surface_copy.wait()
    pieces = []
    for t in range(blocks):
        half = (t % 2) * LANES
        pieces.append(surface_ref[t // 2, :, half : half + LANES].astype(F32))
    sends = []
    for g in range(groups):
        b = g // 2
        if g % 2 == 0:
            source = jnp.where(lane8 < 64, firsts[b], pltpu.roll(seconds[b], 64, 1))
        else:
            source = jnp.where(lane8 < 64, pltpu.roll(firsts[b], 64, 1), seconds[b])
        within = source & (LANES - 1)
        block = source >> 7
        value = jnp.zeros((8, LANES), F32)
        for t in range(blocks):
            value = jnp.where(block == t, lane_pick(pieces[t], within), value)
        value_ref[g] = value.astype(BF16)
        for r in range(copies):
            if g % 4 == 3:
                part = pl.ds(g - 3, 4)
                send = pltpu.make_async_copy(
                    value_ref.at[part], out_hbm.at[part, r], leave.at[g // 4, r]
                )
                send.start()
                sends.append(send)
    within = owner & (LANES - 1)
    box_tile = owner >> 7
    first = jnp.zeros((8, LANES), I32)
    for b in range(box_tiles):
        first = jnp.where(box_tile == b, lane_pick(firsts[b], within), first)
    own_number = iota((8, LANES), 0) * LANES + lane8
    rank = jnp.where(first == own_number, 0, 1)
    spot_ref[...] = (owner >> 6) * LANES + rank * 64 + (owner & 63)
    for send in sends:
        send.wait()


def place(unknowns, owners, groups, copies):
    subs, excitations, _ = unknowns.shape
    return on_chip(
        place_kernel,
        "place",
        "hhhv",
        (unknowns, owners),
        [
            jax.ShapeDtypeStruct((groups, copies, excitations, LANES), BF16),
            jax.ShapeDtypeStruct(owners.shape, I32),
        ],
        scratch=[
            pltpu.VMEM((subs, excitations, owners.size // subs), BF16),
            pltpu.VMEM(owners.shape, I32),
            pltpu.VMEM((groups, excitations, LANES), BF16),
            pltpu.SemaphoreType.DMA((2,)),
            pltpu.SemaphoreType.DMA((groups // 4, copies)),
        ],
        flops=8 * 1024 * 1024,
        moved=300_000,
        room=0,
    )


def slot_order(count_dom, count_dir, transposed):
    size = 2 * count_dom * count_dir
    arrival = iota((size, size), 1 if transposed else 0)
    slot = iota((size, size), 0 if transposed else 1)
    source = arrival & (LANES - 1)
    shift = count_dir.bit_length() - 1
    target = ((source & (count_dir - 1)) * count_dom + (source >> shift)) * 2 + (arrival >> 7)
    return jnp.where(target == slot, 1.0, 0.0).astype(BF16)


def start_copies(source, target, done):
    count = done.shape[0]
    size = source.shape[0] // count
    copies = []
    for m in range(count):
        part = pl.ds(m * size, size)
        copies.append(pltpu.make_async_copy(source.at[part], target.at[part], done.at[m]))
        copies[m].start()
    return copies


def radiate_kernel(counts, arrived_ref, agg_hbm, pattern_ref, current_ref, wide, turned,
                   agg_ref, done):
    boxes, directions, slots = agg_ref.shape
    copies = start_copies(agg_hbm, agg_ref, done)
    excitations = arrived_ref.shape[1]
    tail = directions - LANES
    share = LANES // tail
    wide[...] = arrived_ref[...].astype(F32)
    for e in range(excitations):
        turned[:, e, :] = jnp.transpose(wide[:, e, :])
    first = turned[0:boxes].reshape(boxes * excitations, LANES)
    second = turned[boxes : 2 * boxes].reshape(boxes * excitations, LANES)
    both = jnp.concatenate([first, second], axis=1).astype(BF16)
    ordered = jnp.dot(both, slot_order(*counts, False), preferred_element_type=F32)
    current_ref[...] = ordered.astype(BF16).reshape(boxes, excitations, slots)
    for m in range(boxes // share):
        copies[m].wait()
        tails = []
        for n in range(m * share, (m + 1) * share):
            field = lax.dot_general(
                current_ref[n], agg_ref[n], (((1,), (1,)), ((), ())), preferred_element_type=F32
            )
            pattern_ref[n] = field[:, 0:LANES].astype(BF16)
            tails.append(field[:, LANES:directions])
        pattern_ref[boxes + m] = jnp.concatenate(tails, axis=1).astype(BF16)


def radiate(arrived, agg, counts):
    sources, excitations, width = arrived.shape
    boxes, directions, slots = agg.shape
    packed = boxes * directions // LANES
    return on_chip(
        functools.partial(radiate_kernel, counts),
        "radiate",
        "vhvv",
        (arrived, agg),
        [
            jax.ShapeDtypeStruct((packed, excitations, LANES), BF16),
            jax.ShapeDtypeStruct((boxes, excitations, slots), BF16),
        ],
        scratch=[
            pltpu.VMEM((sources, excitations, width), F32),
            pltpu.VMEM((width, excitations, sources), F32),
            pltpu.VMEM(agg.shape, BF16),
            pltpu.SemaphoreType.DMA((boxes // (LANES // (directions - LANES)),)),
        ],
        flops=2 * boxes * 8 * directions * slots,
        moved=2 * boxes * directions * slots,
    )


def near_kernel(near_ref, current_ref, block_hbm, out_ref, block_ref, done):
    own, count = block_ref.shape[:2]
    copies = start_copies(block_hbm, block_ref, done)
    for n in range(own):
        copies[n].wait()
        total = None
        for j in range(count):
            field = lax.dot_general(
                current_ref[near_ref[j, n]],
                block_ref[n, j],
                (((1,), (1,)), ((), ())),
                preferred_element_type=F32,
            )
            total = field if j == 0 else total + field
        out_ref[n] = total


def near(near_list, current, blocks):
    own, count, slots, _ = blocks.shape
    excitations = current.shape[1]
    return on_chip(
        near_kernel,
        "near",
        "svhv",
        (near_list, current, blocks),
        jax.ShapeDtypeStruct((own, excitations, slots), F32),
        scratch=[pltpu.VMEM(blocks.shape, BF16), pltpu.SemaphoreType.DMA((own,))],
        flops=2 * own * count * 8 * slots * slots,
        moved=2 * own * count * slots * slots,
    )


def schur_kernel(unknown_ref, schur_hbm, out_ref, schur_ref, done):
    subs = unknown_ref.shape[0]
    rows = schur_ref.shape[1]
    cuts = schur_ref.shape[0] // subs
    copies = start_copies(schur_hbm, schur_ref, done)
    for s in range(subs):
        for c in range(cuts):
            copies[s * cuts + c].wait()
            out_ref[s, :, c * rows : (c + 1) * rows] = lax.dot_general(
                unknown_ref[s],
                schur_ref[s * cuts + c],
                (((1,), (1,)), ((), ())),
                preferred_element_type=F32,
            )


def schur(unknowns, schur_blocks, cuts=2):
    subs, width, _ = schur_blocks.shape
    parts = schur_blocks.reshape(subs * cuts, width // cuts, width)
    return on_chip(
        schur_kernel,
        "schur",
        "vhv",
        (unknowns, parts),
        jax.ShapeDtypeStruct(unknowns.shape, F32),
        scratch=[pltpu.VMEM(parts.shape, BF16), pltpu.SemaphoreType.DMA((subs * cuts,))],
        flops=2 * 8 * schur_blocks.size,
        moved=2 * schur_blocks.size,
    )


def couple_kernel(source_ref, before_ref, here_ref, after_ref, map_ref, coupling_ref,
                  schur_ref, out_ref, window):
    subs, links, width = map_ref.shape
    tiles = width // LANES
    window[0:subs] = before_ref[...].astype(F32)
    window[subs : 2 * subs] = here_ref[...].astype(F32)
    window[2 * subs : 3 * subs] = after_ref[...].astype(F32)
    out_ref[...] = schur_ref[...]

    def subdomain(s, carry):
        for k in range(links):
            base = source_ref[s * links + k]
            pieces = [window[base, :, q * LANES : (q + 1) * LANES] for q in range(tiles)]
            for t in range(tiles):
                cut = slice(t * LANES, (t + 1) * LANES)
                rows = jnp.broadcast_to(map_ref[s, k : k + 1, cut], (8, LANES))
                scale = jnp.broadcast_to(coupling_ref[s, k : k + 1, cut], (8, LANES))
                within = rows & (LANES - 1)
                tile = rows >> 7
                value = lane_pick(pieces[0], within)
                for q in range(1, tiles):
                    value = jnp.where(tile == q, lane_pick(pieces[q], within), value)
                out_ref[s, :, cut] += scale * value
        return carry

    lax.fori_loop(0, subs, subdomain, 0)


def couple(sources, before, here, after, row_map, coupling, schur):
    subs, excitations, width = here.shape
    return on_chip(
        couple_kernel,
        "couple",
        "svvvvvvv",
        (sources, before, here, after, row_map, coupling, schur),
        jax.ShapeDtypeStruct(here.shape, F32),
        scratch=[pltpu.VMEM((3 * subs, excitations, width), F32)],
        flops=8 * 1024 * 1024,
        moved=8_000_000,
    )


def receive_kernel(counts, place_ref, kind_ref, own_ref, before_ref, here_ref, after_ref,
                   table_ref, agg_hbm, near_ref, out_ref, nearby, result, turned, agg_ref, done):
    boxes, directions, slots = agg_ref.shape
    copies = start_copies(agg_hbm, agg_ref, done)
    excitations = here_ref.shape[1]
    length = place_ref.shape[0]
    tail = directions - LANES
    share = LANES // tail
    own_boxes = near_ref.shape[0]

    for w, source in enumerate((before_ref, here_ref, after_ref)):
        for m in range(boxes // share):
            tails = source[boxes + m].astype(F32)
            for k in range(share):
                n = m * share + k
                row = (w * boxes + n) * 16
                nearby[row : row + 8, :] = source[n].astype(F32)
                turn = (LANES - k * tail) % LANES
                nearby[row + 8 : row + 16, :] = pltpu.roll(tails, turn, 1) if turn else tails

    for n in range(boxes):
        head_sum = None
        tail_sum = None
        for j in range(length):
            spot = pl.multiple_of(place_ref[j, n], 16)
            kind = kind_ref[j, n]
            head = nearby[pl.ds(spot, 8), :] * table_ref[pl.ds(kind, 1), :]
            rest = nearby[pl.ds(spot + 8, 8), :] * table_ref[pl.ds(kind + 1, 1), :]
            head_sum = head if j == 0 else head_sum + head
            tail_sum = rest if j == 0 else tail_sum + rest
        incoming = jnp.concatenate([head_sum, tail_sum[:, 0:tail]], axis=1).astype(BF16)
        if n % share == 0:
            copies[n // share].wait()
        field = jnp.dot(incoming, agg_ref[n], preferred_element_type=F32)
        mine = (own_ref[0] == n // own_boxes).astype(F32)
        field = field + mine * near_ref[n % own_boxes]
        result[n] = field.astype(BF16)

    flat = result[...].reshape(boxes * excitations, slots)
    ordered = jnp.dot(flat, slot_order(*counts, True), preferred_element_type=F32)
    turned[0:boxes] = ordered[:, 0:LANES].reshape(boxes, excitations, LANES)
    turned[boxes : 2 * boxes] = ordered[:, LANES:].reshape(boxes, excitations, LANES)
    pieces = [jnp.transpose(turned[:, e, :]) for e in range(excitations)]
    for e in range(excitations):
        turned[:, e, :] = pieces[e]
    out_ref[...] = turned[...].astype(BF16)


def receive(places, kinds, own, before, here, after, table, agg, near_part, counts):
    boxes, directions, slots = agg.shape
    excitations = here.shape[1]
    targets = slots // 2
    return on_chip(
        functools.partial(receive_kernel, counts),
        "receive",
        "sssvvvvhvv",
        (places, kinds, own, before, here, after, table, agg, near_part),
        jax.ShapeDtypeStruct((targets, excitations, 2 * boxes), BF16),
        scratch=[
            pltpu.VMEM((3 * boxes * 16, LANES), F32),
            pltpu.VMEM((boxes, excitations, slots), BF16),
            pltpu.VMEM((targets, excitations, 2 * boxes), F32),
            pltpu.VMEM(agg.shape, BF16),
            pltpu.SemaphoreType.DMA((boxes // (LANES // (directions - LANES)),)),
        ],
        flops=2 * boxes * 8 * directions * slots,
        moved=2 * boxes * directions * slots,
    )


def finish_kernel(copies, term_ref, spot_ref, base_ref, out_ref):
    groups = term_ref.shape[0] // copies
    fields = []
    for g in range(groups):
        total = term_ref[g * copies].astype(F32)
        for k in range(1, copies):
            total = total + term_ref[g * copies + k].astype(F32)
        fields.append(total.astype(BF16).astype(F32))
    out_ref[...] = base_ref[...]
    for t in range(spot_ref.shape[0]):
        spot = jnp.broadcast_to(spot_ref[t : t + 1, :], (8, LANES))
        within = spot & (LANES - 1)
        group = spot >> 7
        value = lane_pick(fields[0], within)
        for g in range(1, groups):
            value = jnp.where(group == g, lane_pick(fields[g], within), value)
        half = (t % 2) * LANES
        out_ref[t // 2, :, half : half + LANES] += value


def finish(terms, spots, base, copies):
    return on_chip(
        functools.partial(finish_kernel, copies),
        "finish",
        "vvvv",
        (terms, spots, base),
        jax.ShapeDtypeStruct(base.shape, F32),
        flops=8 * 1024 * 128,
        moved=600_000,
    )


def both_ways(value, axis):
    count = lax.axis_size(axis)
    up = [(i, (i + 1) % count) for i in range(count)]
    down = [(j, i) for i, j in up]
    return lax.ppermute(value, axis, up), lax.ppermute(value, axis, down)


def exchange(value):
    return lax.all_to_all(value, ("dom", "dir"), split_axis=0, concat_axis=0, tiled=True)


def shards(unknowns, schur_blocks, adjacency, row_map, coupling, owner_box, aggregation,
           trans_table, inter_list, inter_type, near_list, near_blocks):
    doms = lax.axis_size("dom")
    dirs = lax.axis_size("dir")
    dom_here = lax.axis_index("dom")
    dir_here = lax.axis_index("dir")
    counts = (doms, dirs)
    subs, excitations, _ = unknowns.shape
    group = aggregation.shape[0]
    agg = jnp.swapaxes(aggregation, 1, 2)

    owners = owner_box.reshape(-1, LANES)
    placed, spots = place(unknowns, owners, doms, dirs)
    arrived = exchange(placed.reshape(doms * dirs, excitations, 2 * group))

    before_u, after_u = both_ways(unknowns, "dom")
    schur_part = schur(unknowns, schur_blocks)
    source_dom = adjacency // (subs * dirs)
    links = ((source_dom - dom_here + 1 + doms) % doms) * subs + adjacency % subs
    listed = inter_list.T
    places = (((listed // group - dom_here + 1 + doms) % doms) * group + listed % group) * 16
    kinds = inter_type.T * 2
    table = jnp.pad(trans_table, ((0, 0), (0, 2 * LANES - trans_table.shape[1])))
    table = table.reshape(-1, LANES)
    arrived, schur_part, places, kinds, table, before_u, after_u = lax.optimization_barrier(
        (arrived, schur_part, places, kinds, table, before_u, after_u)
    )

    patterns, current = radiate(arrived, agg, counts)
    before_p, after_p = both_ways(patterns, "dom")
    near_part = near(near_list.T, current, near_blocks)
    terms = receive(places, kinds, dir_here.reshape(1), before_p, patterns, after_p,
                    table, agg, near_part, counts)
    terms, before_u, after_u = lax.optimization_barrier((terms, before_u, after_u))
    base = couple(links.reshape(-1), before_u, unknowns, after_u, row_map, coupling, schur_part)
    gathered = exchange(terms)
    return finish(gathered, spots, base, dirs)


def solution(mesh):
    split = ("dom", "dir")
    in_specs = (
        P(split, None, None),
        P(split, None, None),
        P(split, None),
        P(split, None, None),
        P(split, None, None),
        P(split, None, None),
        P("dom", None, "dir"),
        P(None, "dir"),
        P("dom", None),
        P("dom", None),
        P(split, None),
        P(split, None, None, None),
    )
    out_specs = P(split, None, None)
    return jax.shard_map(shards, mesh=mesh, in_specs=in_specs, out_specs=out_specs, check_vma=False)
```

time: 79.1 us -> 66.9 us (0.85)
  waiting for transfers between devices: 3.93 us -> 14.5 us
  local copies, waits for them, and re-layouts: 9.51 us -> 2.08 us
  matrix products: 6.31 us -> 0 us
  Pallas kernels: 31 us -> 26.1 us
  starting transfers between devices: 26.7 us -> 22.1 us
    all_to_all x2, waiting for transfers between devices: 3.92 us -> 11.3 us  [exchange(): lax.all_to_all(value, ('dom', 'dir'), split_axis=0, concat_axis=0, tiled=...]
    dot_general x1 -> x0, matrix products: 6.31 us -> none  [shards(): jnp.einsum('sij,sej->sei', schur_blocks, unknowns, preferred_element_type...]
    pallas_call x6 -> x7, Pallas kernels: 31 us -> 26.1 us  [on_chip(): pl.pallas_call(kernel, in_specs=specs[:count], out_specs=specs[count:] if...]
    unnamed x19 -> x15, local copies, waits for them, and re-layouts: 6.75 us -> 1.95 us
    all_to_all x2, starting transfers between devices: 16.2 us -> 12.6 us  [exchange(): lax.all_to_all(value, ('dom', 'dir'), split_axis=0, concat_axis=0, tiled=...]
    ppermute x4, waiting for transfers between devices: 0.01 us -> 3.23 us  [both_ways(): return (lax.ppermute(value, axis, up), lax.ppermute(value, axis, down))]
    reshape x3 -> x1, local copies, waits for them, and re-layouts: 2 us -> 0.02 us  [shards(): table = table.reshape(-1, LANES)]
    mul x0 -> x2, other arithmetic: none -> 1.42 us  [the longest x1 0.72 us: shards(): ((listed // group - dom_here + 1 + doms) % doms * group + listed % group)...]
  transfers between devices with their start and end apart: 6 -> 6, of which waited for: 1 -> 3; matrix products, arithmetic and copies ran while one was open for 17% -> 4% of each run, Pallas kernels for 34% -> 23%
where the time goes in v1:
time: 66.9 us; the launch traced here: 66.4 us
  Pallas kernels  26.1 us (39%)
  starting transfers between devices  22.1 us (33%)
  waiting for transfers between devices  14.5 us (22%)
  local copies, waits for them, and re-layouts  2.08 us (3%)
  other arithmetic  1.44 us (2%)
    pallas_call x7, Pallas kernels, on_chip(): pl.pallas_call(kernel, in_specs=specs[:count], out_specs=specs[count:] if...  26.1 us
    all_to_all x2, starting transfers between devices, exchange(): lax.all_to_all(value, ('dom', 'dir'), split_axis=0, concat_axis=0, tiled=...  12.6 us
    all_to_all x2, waiting for transfers between devices, exchange(): lax.all_to_all(value, ('dom', 'dir'), split_axis=0, concat_axis=0, tiled=...  11.3 us
    ppermute x4, starting transfers between devices, both_ways(): return (lax.ppermute(value, axis, up), lax.ppermute(value, axis, down))  9.5 us
    ppermute x4, waiting for transfers between devices, both_ways(): return (lax.ppermute(value, axis, up), lax.ppermute(value, axis, down))  3.23 us
    unnamed x15, local copies, waits for them, and re-layouts  1.95 us
  transfers between devices with their start and end apart: 6, of which 3 were waited for; matrix products, arithmetic and copies ran while one was open for 4% of the time, Pallas kernels for 23%

profile of v1, /device:TPU:1, one launch (start us, length us, event | category | flops | bytes accessed | tf_op | source)
XLA Modules:
  0.0 66.4 jit_solution(17037040611615170182)
XLA Ops:
  0.0 2.5 %collective-permute-start = (bf16[4,8,1024]{2,1,0:T(8,128)(2,1)}, bf16[4,8,1024]{2,1,0:T(8,128)(2,1)}, u32[]{:S(2)}, u32[]{:S(2)}) collective-permute-start(bf16[4,8,1024]{2,1,0:T(8,128)(2,1)} %here_ref.1), channel_id=1, source_target_pairs={{0,8},{8,16},{16,24},{24,32},{32,40},{40,48},{48,56},{56,64},{64,7... | collective-permute-start | bytes 196616 | tf_op jit(solution)/shard_map/ppermute | solution.py:429
  2.5 4.6 %collective-permute-start.1 = (bf16[4,8,1024]{2,1,0:T(8,128)(2,1)}, bf16[4,8,1024]{2,1,0:T(8,128)(2,1)}, u32[]{:S(2)}, u32[]{:S(2)}) collective-permute-start(bf16[4,8,1024]{2,1,0:T(8,128)(2,1)} %here_ref.1), channel_id=1, source_target_pairs={{8,0},{16,8},{24,16},{32,24},{40,32},{48,40},{56,48},{64,56},{72,6... | collective-permute-start | bytes 196616 | tf_op jit(solution)/shard_map/ppermute | solution.py:429
  7.0 3.4 %place.1 = (bf16[16,8,8,128]{3,2,1,0:T(8,128)(2,1)}, s32[8,128]{1,0:T(8,128)}) custom-call(bf16[4,8,1024]{2,1,0:T(8,128)(2,1)} %here_ref.1, s32[8,128]{1,0:T(8,128)} %bitcast.31), custom_call_target="tpu_custom_call" | custom-call | flops 8388608 | bytes 300000 | tf_op jit(solution)/shard_map/place/pallas_call | solution.py:35
  10.4 6.5 %all-to-all-start = ((bf16[128,8,128]{2,1,0:T(8,128)(2,1)}), bf16[128,8,128]{2,1,0:T(8,128)(2,1)S(1)}, u32[]{:S(2)}, u32[]{:S(2)}) async-start(bf16[128,8,128]{2,1,0:T(8,128)(2,1)} %bitcast.30), calls=%async_computation | async-start | bytes 524288 | tf_op jit(solution)/shard_map/all_to_all | solution.py:433
  16.9 0.7 %multiply_bitcast_fusion.kind_ref = s32[16,64]{1,0:T(8,128)S(1)} fusion(s32[64,16]{0,1:T(8,128)} %param.21), kind=kLoop, calls=%fused_computation.17 | loop fusion | flops 1024 | bytes 8192 | tf_op jit(solution)/shard_map/mul | solution.py:457
  17.6 0.7 %fusion.5.place_ref = s32[16,64]{1,0:T(8,128)S(1)} fusion(s32[64,16]{0,1:T(8,128)} %param.20, s32[]{:T(128)S(6)} %axis_index.23), kind=kLoop, calls=%fused_computation.13 | loop fusion | flops 35840 | bytes 8196 | tf_op jit(solution)/shard_map/mul | solution.py:456
  18.3 1.1 %copy.14 = f32[316,144]{1,0:T(8,128)S(1)} copy(f32[316,144]{0,1:T(8,128)} %param.19) | data formatting | bytes 364032
  19.5 0.0 copy-start
  19.5 0.8 %copy-done = bf16[4,8,1024]{2,1,0:T(8,128)(2,1)S(1)} copy-done((bf16[4,8,1024]{2,1,0:T(8,128)(2,1)S(1)}, bf16[4,8,1024]{2,1,0:T(8,128)(2,1)}, u32[]{:S(2)}) %copy-start) | copy-done | bytes 65560
  20.3 0.0 copy-start.5
  20.3 4.4 %schur.1.schur_ref = f32[4,8,1024]{2,1,0:T(8,128)S(1)} custom-call(bf16[4,8,1024]{2,1,0:T(8,128)(2,1)S(1)} %copy-done, bf16[8,512,1024]{2,1,0:T(8,128)(2,1)} %bitcast.29), custom_call_target="tpu_custom_call" | custom-call | flops 67108864 | bytes 8388608 | tf_op jit(solution)/shard_map/schur/pallas_call | solution.py:35
  24.7 0.0 collective-permute-done.before_ref
  24.8 0.0 collective-permute-done.1.after_ref
  24.8 3.2 %all-to-all-done.arrived_ref = bf16[128,8,128]{2,1,0:T(8,128)(2,1)S(1)} async-done(((bf16[128,8,128]{2,1,0:T(8,128)(2,1)}), bf16[128,8,128]{2,1,0:T(8,128)(2,1)S(1)}, u32[]{:S(2)}, u32[]{:S(2)}) %all-to-all-start) | async-done | bytes 262176 | tf_op jit(solution)/shard_map/all_to_all | solution.py:433
  27.9 3.9 %radiate.1 = (bf16[72,8,128]{2,1,0:T(8,128)(2,1)S(1)}, bf16[64,8,256]{2,1,0:T(8,128)(2,1)S(1)}) custom-call(bf16[128,8,128]{2,1,0:T(8,128)(2,1)S(1)} %all-to-all-done.arrived_ref, bf16[64,144,256]{2,1,0:T(8,128)(2,1)} %bitcast.27), custom_call_target="tpu_custom_call" | custom-call | flops 37748736 | bytes 4718592 | tf_op jit(solution)/shard_map/radiate/pallas_call | solution.py:35
  31.8 2.5 %collective-permute-start.3 = (bf16[72,8,128]{2,1,0:T(8,128)(2,1)S(1)}, bf16[72,8,128]{2,1,0:T(8,128)(2,1)S(1)}, u32[]{:S(2)}, u32[]{:S(2)}) collective-permute-start(bf16[72,8,128]{2,1,0:T(8,128)(2,1)S(1)} %get-tuple-element.23.here_ref), channel_id=1, source_target_pairs={{8,0},{16,8},{24,16},{32,24},{40,32},{48,40},{56,48},{64,56},{72,6... | collective-permute-start | bytes 442376 | tf_op jit(solution)/shard_map/ppermute | solution.py:429
  34.3 0.0 collective-permute-start.2
  34.3 0.0 copy-done.5
  34.3 0.0 copy-start.6
  34.3 0.0 copy-start.1
  34.3 0.0 copy-start.2
  34.3 0.0 copy-start.3
  34.3 0.0 copy-start.4
  34.4 4.8 %near.1.near_ref = f32[8,8,256]{2,1,0:T(8,128)S(1)} custom-call(s32[4,8]{1,0:T(4,128)S(1)} %bitcast.26, bf16[64,8,256]{2,1,0:T(8,128)(2,1)S(1)} %get-tuple-element.25.current_ref, bf16[8,4,256,256]{3,2,1,0:T(8,128)(2,1)} %block_hbm.1), custom_call_target="tpu_custom_call" | custom-call | flops 33554432 | bytes 4194304 | tf_op jit(solution)/shard_map/near/pallas_call | solution.py:35
  39.1 0.0 collective-permute-done.3.after_ref
  39.1 3.2 %collective-permute-done.2.before_ref = bf16[72,8,128]{2,1,0:T(8,128)(2,1)S(1)} collective-permute-done((bf16[72,8,128]{2,1,0:T(8,128)(2,1)S(1)}, bf16[72,8,128]{2,1,0:T(8,128)(2,1)S(1)}, u32[]{:S(2)}, u32[]{:S(2)}) %collective-permute-start.2) | collective-permute-done | bytes 147488 | tf_op jit(solution)/shard_map/ppermute | solution.py:429
  42.4 6.1 %receive.1 = bf16[128,8,128]{2,1,0:T(8,128)(2,1)} custom-call(s32[16,64]{1,0:T(8,128)S(1)} %fusion.5.place_ref, s32[16,64]{1,0:T(8,128)S(1)} %multiply_bitcast_fusion.kind_ref, s32[1]{0:T(128)} %bitcast.5.own_ref, bf16[72,8,128]{2,1,0:T(8,128)(2,1)S(1)} %collective-permute-done.2.before_ref, bf16[72,8,128]{2,1,0:T(8,128)(2,1)S(1)} %get-tuple-element.23.here_ref, ...), custom_call_target="tpu_custom_call" | custom-call | flops 37748736 | bytes 4718592 | tf_op jit(solution)/shard_map/receive/pallas_call | solution.py:35
  48.5 6.1 %all-to-all-start.1 = ((bf16[128,8,128]{2,1,0:T(8,128)(2,1)}), bf16[128,8,128]{2,1,0:T(8,128)(2,1)S(1)}, u32[]{:S(2)}, u32[]{:S(2)}) async-start(bf16[128,8,128]{2,1,0:T(8,128)(2,1)} %receive.1), calls=%async_computation.1 | async-start | bytes 524288 | tf_op jit(solution)/shard_map/all_to_all | solution.py:433
  54.6 0.0 copy-done.6
  54.6 0.1 reshape.23.source_ref
  54.7 0.0 copy-done.1
  54.7 0.0 copy-done.2
  54.7 0.0 copy-done.3
  54.7 2.8 %couple.1.base_ref = f32[4,8,1024]{2,1,0:T(8,128)S(1)} custom-call(s32[16]{0:T(128)S(1)} %reshape.23.source_ref, bf16[4,8,1024]{2,1,0:T(8,128)(2,1)} %collective-permute-done.before_ref, bf16[4,8,1024]{2,1,0:T(8,128)(2,1)S(1)} %copy-done.1, bf16[4,8,1024]{2,1,0:T(8,128)(2,1)} %collective-permute-done.1.after_ref, s32[4,4,1024]{2,1,0:T(4,128)S(1)} %copy-done.2, ...), custom_call_target="tpu_custom_call" | custom-call | flops 8388608 | bytes 8000000 | tf_op jit(solution)/shard_map/couple/pallas_call | solution.py:35
  57.5 8.1 %all-to-all-done.1.term_ref = bf16[128,8,128]{2,1,0:T(8,128)(2,1)S(1)} async-done(((bf16[128,8,128]{2,1,0:T(8,128)(2,1)}), bf16[128,8,128]{2,1,0:T(8,128)(2,1)S(1)}, u32[]{:S(2)}, u32[]{:S(2)}) %all-to-all-start.1) | async-done | bytes 262176 | tf_op jit(solution)/shard_map/all_to_all | solution.py:433
  65.6 0.0 copy-done.4
  65.6 0.8 %finish.1 = f32[4,8,1024]{2,1,0:T(8,128)} custom-call(bf16[128,8,128]{2,1,0:T(8,128)(2,1)S(1)} %all-to-all-done.1.term_ref, s32[8,128]{1,0:T(8,128)S(1)} %copy-done.4, f32[4,8,1024]{2,1,0:T(8,128)S(1)} %couple.1.base_ref), custom_call_target="tpu_custom_call" | custom-call | flops 1048576 | bytes 600000 | tf_op jit(solution)/shard_map/finish/pallas_call | solution.py:35
  (3 shorter events, 0.1 us)
Async XLA Ops:
  0.0 24.7 %collective-permute-start = (bf16[4,8,1024]{2,1,0:T(8,128)(2,1)}, bf16[4,8,1024]{2,1,0:T(8,128)(2,1)}, u32[]{:S(2)}, u32[]{:S(2)}) collective-permute-start(bf16[4,8,1024]{2,1,0:T(8,128)(2,1)} %here_ref.1), channel_id=1, source_target_pairs={{0,8},{8,16},{16,24},{24,32},{32,40},{40,48},{48,56},{56,64},{64,7... | collective-permute-start | bytes 196616 | tf_op jit(solution)/shard_map/ppermute | solution.py:429
  2.5 22.3 %collective-permute-start.1 = (bf16[4,8,1024]{2,1,0:T(8,128)(2,1)}, bf16[4,8,1024]{2,1,0:T(8,128)(2,1)}, u32[]{:S(2)}, u32[]{:S(2)}) collective-permute-start(bf16[4,8,1024]{2,1,0:T(8,128)(2,1)} %here_ref.1), channel_id=1, source_target_pairs={{8,0},{16,8},{24,16},{32,24},{40,32},{48,40},{56,48},{64,56},{72,6... | collective-permute-start | bytes 196616 | tf_op jit(solution)/shard_map/ppermute | solution.py:429
  10.4 17.5 %all-to-all-start = ((bf16[128,8,128]{2,1,0:T(8,128)(2,1)}), bf16[128,8,128]{2,1,0:T(8,128)(2,1)S(1)}, u32[]{:S(2)}, u32[]{:S(2)}) async-start(bf16[128,8,128]{2,1,0:T(8,128)(2,1)} %bitcast.30), calls=%async_computation | async-start | bytes 524288 | tf_op jit(solution)/shard_map/all_to_all | solution.py:433
  19.5 0.8 %copy-start = (bf16[4,8,1024]{2,1,0:T(8,128)(2,1)S(1)}, bf16[4,8,1024]{2,1,0:T(8,128)(2,1)}, u32[]{:S(2)}) copy-start(bf16[4,8,1024]{2,1,0:T(8,128)(2,1)} %here_ref.1) | copy-start | bytes 196612
  20.3 14.0 %copy-start.5 = (s32[8,4]{0,1:T(4,128)S(1)}, s32[8,4]{0,1:T(4,128)}, u32[]{:S(2)}) copy-start(s32[8,4]{0,1:T(4,128)} %param.22) | copy-start | bytes 388
  31.8 7.3 %collective-permute-start.3 = (bf16[72,8,128]{2,1,0:T(8,128)(2,1)S(1)}, bf16[72,8,128]{2,1,0:T(8,128)(2,1)S(1)}, u32[]{:S(2)}, u32[]{:S(2)}) collective-permute-start(bf16[72,8,128]{2,1,0:T(8,128)(2,1)S(1)} %get-tuple-element.23.here_ref), channel_id=1, source_target_pairs={{8,0},{16,8},{24,16},{32,24},{40,32},{48,40},{56,48},{64,56},{72,6... | collective-permute-start | bytes 442376 | tf_op jit(solution)/shard_map/ppermute | solution.py:429
  34.3 8.1 %collective-permute-start.2 = (bf16[72,8,128]{2,1,0:T(8,128)(2,1)S(1)}, bf16[72,8,128]{2,1,0:T(8,128)(2,1)S(1)}, u32[]{:S(2)}, u32[]{:S(2)}) collective-permute-start(bf16[72,8,128]{2,1,0:T(8,128)(2,1)S(1)} %get-tuple-element.23.here_ref), channel_id=1, source_target_pairs={{0,8},{8,16},{16,24},{24,32},{32,40},{40,48},{48,56},{56,64},{64,7... | collective-permute-start | bytes 442376 | tf_op jit(solution)/shard_map/ppermute | solution.py:429
  34.3 20.3 %copy-start.6 = (s32[4,4]{1,0:T(4,128)S(1)}, s32[4,4]{1,0:T(4,128)}, u32[]{:S(2)}) copy-start(s32[4,4]{1,0:T(4,128)} %param.14) | copy-start | bytes 196
  34.3 20.4 %copy-start.1 = (bf16[4,8,1024]{2,1,0:T(8,128)(2,1)S(1)}, bf16[4,8,1024]{2,1,0:T(8,128)(2,1)}, u32[]{:S(2)}) copy-start(bf16[4,8,1024]{2,1,0:T(8,128)(2,1)} %here_ref.1) | copy-start | bytes 196612
  34.3 20.4 %copy-start.2 = (s32[4,4,1024]{2,1,0:T(4,128)S(1)}, s32[4,4,1024]{2,1,0:T(4,128)}, u32[]{:S(2)}) copy-start(s32[4,4,1024]{2,1,0:T(4,128)} %map_ref.1) | copy-start | bytes 196612
  34.3 20.4 %copy-start.3 = (f32[4,4,1024]{2,1,0:T(4,128)S(1)}, f32[4,4,1024]{2,1,0:T(4,128)}, u32[]{:S(2)}) copy-start(f32[4,4,1024]{2,1,0:T(4,128)} %coupling_ref.1) | copy-start | bytes 196612
  34.3 31.2 %copy-start.4 = (s32[8,128]{1,0:T(8,128)S(1)}, s32[8,128]{1,0:T(8,128)}, u32[]{:S(2)}) copy-start(s32[8,128]{1,0:T(8,128)} %get-tuple-element.29.spot_ref) | copy-start | bytes 12292
  48.5 17.1 %all-to-all-start.1 = ((bf16[128,8,128]{2,1,0:T(8,128)(2,1)}), bf16[128,8,128]{2,1,0:T(8,128)(2,1)S(1)}, u32[]{:S(2)}, u32[]{:S(2)}) async-start(bf16[128,8,128]{2,1,0:T(8,128)(2,1)} %receive.1), calls=%async_computation.1 | async-start | bytes 524288 | tf_op jit(solution)/shard_map/all_to_all | solution.py:433

commit v2 on v1

--- a/solution.py
+++ b/solution.py
@@ -7,6 +7,7 @@
 from jax.experimental.pallas import tpu as pltpu
 from jax.sharding import PartitionSpec as P
 
+
 F32 = jnp.float32
 BF16 = jnp.bfloat16
 I32 = jnp.int32
@@ -28,7 +29,7 @@
 MIB = 1024 * 1024
 
 
-def on_chip(kernel, name, spaces, operands, outputs, scratch=(), flops=0, moved=0, room=12 * MIB):
+def on_chip(kernel, spaces, operands, outputs, scratch=(), flops=0, moved=0, room=12 * MIB):
     specs = [{"s": SMEM_SPEC, "v": VMEM_SPEC, "h": HBM_SPEC}[c] for c in spaces]
     count = len(operands)
     several = isinstance(outputs, list)
@@ -40,7 +41,6 @@
         scratch_shapes=list(scratch),
         compiler_params=pltpu.CompilerParams(vmem_limit_bytes=VMEM_BYTES - room),
         cost_estimate=pl.CostEstimate(flops=flops, bytes_accessed=moved, transcendentals=0),
-        name=name,
     )(*operands)
 
 
@@ -123,7 +123,6 @@
     subs, excitations, _ = unknowns.shape
     return on_chip(
         place_kernel,
-        "place",
         "hhhv",
         (unknowns, owners),
         [
@@ -153,21 +152,29 @@
     return jnp.where(target == slot, 1.0, 0.0).astype(BF16)
 
 
-def start_copies(source, target, done):
-    count = done.shape[0]
-    size = source.shape[0] // count
-    copies = []
-    for m in range(count):
-        part = pl.ds(m * size, size)
-        copies.append(pltpu.make_async_copy(source.at[part], target.at[part], done.at[m]))
-        copies[m].start()
-    return copies
-
-
-def radiate_kernel(counts, arrived_ref, agg_hbm, pattern_ref, current_ref, wide, turned,
-                   agg_ref, done):
+class Stream:
+    def __init__(self, source, target, done, depth):
+        size = source.shape[0] // done.shape[0]
+        self.depth = depth
+        self.copies = []
+        for m in range(done.shape[0]):
+            part = pl.ds(m * size, size)
+            self.copies.append(
+                pltpu.make_async_copy(source.at[part], target.at[part], done.at[m])
+            )
+        for copy in self.copies[:depth]:
+            copy.start()
+
+    def take(self, m):
+        self.copies[m].wait()
+        if m + self.depth < len(self.copies):
+            self.copies[m + self.depth].start()
+
+
+def radiate_kernel(counts, arrived_ref, agg_hbm, pattern_ref, current_ref, agg_ref, wide, turned,
+                   done):
     boxes, directions, slots = agg_ref.shape
-    copies = start_copies(agg_hbm, agg_ref, done)
+    stream = Stream(agg_hbm, agg_ref, done, 4)
     excitations = arrived_ref.shape[1]
     tail = directions - LANES
     share = LANES // tail
@@ -180,7 +187,7 @@
     ordered = jnp.dot(both, slot_order(*counts, False), preferred_element_type=F32)
     current_ref[...] = ordered.astype(BF16).reshape(boxes, excitations, slots)
     for m in range(boxes // share):
-        copies[m].wait()
+        stream.take(m)
         tails = []
         for n in range(m * share, (m + 1) * share):
             field = lax.dot_general(
@@ -197,29 +204,29 @@
     packed = boxes * directions // LANES
     return on_chip(
         functools.partial(radiate_kernel, counts),
-        "radiate",
-        "vhvv",
+        "vhvvv",
         (arrived, agg),
         [
             jax.ShapeDtypeStruct((packed, excitations, LANES), BF16),
             jax.ShapeDtypeStruct((boxes, excitations, slots), BF16),
+            jax.ShapeDtypeStruct(agg.shape, BF16),
         ],
         scratch=[
             pltpu.VMEM((sources, excitations, width), F32),
             pltpu.VMEM((width, excitations, sources), F32),
-            pltpu.VMEM(agg.shape, BF16),
             pltpu.SemaphoreType.DMA((boxes // (LANES // (directions - LANES)),)),
         ],
         flops=2 * boxes * 8 * directions * slots,
         moved=2 * boxes * directions * slots,
+        room=16 * MIB,
     )
 
 
 def near_kernel(near_ref, current_ref, block_hbm, out_ref, block_ref, done):
     own, count = block_ref.shape[:2]
-    copies = start_copies(block_hbm, block_ref, done)
+    stream = Stream(block_hbm, block_ref, done, 4)
     for n in range(own):
-        copies[n].wait()
+        stream.take(n)
         total = None
         for j in range(count):
             field = lax.dot_general(
@@ -237,11 +244,11 @@
     excitations = current.shape[1]
     return on_chip(
         near_kernel,
-        "near",
         "svhv",
         (near_list, current, blocks),
         jax.ShapeDtypeStruct((own, excitations, slots), F32),
         scratch=[pltpu.VMEM(blocks.shape, BF16), pltpu.SemaphoreType.DMA((own,))],
+        room=16 * MIB,
         flops=2 * own * count * 8 * slots * slots,
         moved=2 * own * count * slots * slots,
     )
@@ -251,10 +258,10 @@
     subs = unknown_ref.shape[0]
     rows = schur_ref.shape[1]
     cuts = schur_ref.shape[0] // subs
-    copies = start_copies(schur_hbm, schur_ref, done)
+    stream = Stream(schur_hbm, schur_ref, done, 4)
     for s in range(subs):
         for c in range(cuts):
-            copies[s * cuts + c].wait()
+            stream.take(s * cuts + c)
             out_ref[s, :, c * rows : (c + 1) * rows] = lax.dot_general(
                 unknown_ref[s],
                 schur_ref[s * cuts + c],
@@ -268,7 +275,6 @@
     parts = schur_blocks.reshape(subs * cuts, width // cuts, width)
     return on_chip(
         schur_kernel,
-        "schur",
         "vhv",
         (unknowns, parts),
         jax.ShapeDtypeStruct(unknowns.shape, F32),
@@ -310,7 +316,6 @@
     subs, excitations, width = here.shape
     return on_chip(
         couple_kernel,
-        "couple",
         "svvvvvvv",
         (sources, before, here, after, row_map, coupling, schur),
         jax.ShapeDtypeStruct(here.shape, F32),
@@ -321,9 +326,8 @@
 
 
 def receive_kernel(counts, place_ref, kind_ref, own_ref, before_ref, here_ref, after_ref,
-                   table_ref, agg_hbm, near_ref, out_ref, nearby, result, turned, agg_ref, done):
+                   table_ref, agg_ref, near_ref, out_ref, nearby, result, turned):
     boxes, directions, slots = agg_ref.shape
-    copies = start_copies(agg_hbm, agg_ref, done)
     excitations = here_ref.shape[1]
     length = place_ref.shape[0]
     tail = directions - LANES
@@ -351,12 +355,9 @@
             head_sum = head if j == 0 else head_sum + head
             tail_sum = rest if j == 0 else tail_sum + rest
         incoming = jnp.concatenate([head_sum, tail_sum[:, 0:tail]], axis=1).astype(BF16)
-        if n % share == 0:
-            copies[n // share].wait()
         field = jnp.dot(incoming, agg_ref[n], preferred_element_type=F32)
         mine = (own_ref[0] == n // own_boxes).astype(F32)
-        field = field + mine * near_ref[n % own_boxes]
-        result[n] = field.astype(BF16)
+        result[n] = (field + mine * near_ref[n % own_boxes]).astype(BF16)
 
     flat = result[...].reshape(boxes * excitations, slots)
     ordered = jnp.dot(flat, slot_order(*counts, True), preferred_element_type=F32)
@@ -374,19 +375,17 @@
     targets = slots // 2
     return on_chip(
         functools.partial(receive_kernel, counts),
-        "receive",
-        "sssvvvvhvv",
+        "sssvvvvvvv",
         (places, kinds, own, before, here, after, table, agg, near_part),
         jax.ShapeDtypeStruct((targets, excitations, 2 * boxes), BF16),
         scratch=[
             pltpu.VMEM((3 * boxes * 16, LANES), F32),
             pltpu.VMEM((boxes, excitations, slots), BF16),
             pltpu.VMEM((targets, excitations, 2 * boxes), F32),
-            pltpu.VMEM(agg.shape, BF16),
-            pltpu.SemaphoreType.DMA((boxes // (LANES // (directions - LANES)),)),
         ],
         flops=2 * boxes * 8 * directions * slots,
         moved=2 * boxes * directions * slots,
+        room=16 * MIB,
     )
 
 
@@ -413,7 +412,6 @@
 def finish(terms, spots, base, copies):
     return on_chip(
         functools.partial(finish_kernel, copies),
-        "finish",
         "vvvv",
         (terms, spots, base),
         jax.ShapeDtypeStruct(base.shape, F32),
@@ -449,7 +447,6 @@
     arrived = exchange(placed.reshape(doms * dirs, excitations, 2 * group))
 
     before_u, after_u = both_ways(unknowns, "dom")
-    schur_part = schur(unknowns, schur_blocks)
     source_dom = adjacency // (subs * dirs)
     links = ((source_dom - dom_here + 1 + doms) % doms) * subs + adjacency % subs
     listed = inter_list.T
@@ -457,16 +454,20 @@
     kinds = inter_type.T * 2
     table = jnp.pad(trans_table, ((0, 0), (0, 2 * LANES - trans_table.shape[1])))
     table = table.reshape(-1, LANES)
-    arrived, schur_part, places, kinds, table, before_u, after_u = lax.optimization_barrier(
-        (arrived, schur_part, places, kinds, table, before_u, after_u)
-    )
-
-    patterns, current = radiate(arrived, agg, counts)
+    dir_here = dir_here.reshape(1)
+    arrived, places, kinds, table, before_u, after_u, dir_here = lax.optimization_barrier(
+        (arrived, places, kinds, table, before_u, after_u, dir_here)
+    )
+
+    patterns, current, agg = radiate(arrived, agg, counts)
     before_p, after_p = both_ways(patterns, "dom")
     near_part = near(near_list.T, current, near_blocks)
-    terms = receive(places, kinds, dir_here.reshape(1), before_p, patterns, after_p,
+    terms = receive(places, kinds, dir_here, before_p, patterns, after_p,
                     table, agg, near_part, counts)
-    terms, before_u, after_u = lax.optimization_barrier((terms, before_u, after_u))
+    terms, before_u, after_u, unknowns = lax.optimization_barrier(
+        (terms, before_u, after_u, unknowns)
+    )
+    schur_part = schur(unknowns, schur_blocks)
     base = couple(links.reshape(-1), before_u, unknowns, after_u, row_map, coupling, schur_part)
     gathered = exchange(terms)
     return finish(gathered, spots, base, dirs)

time: 66.9 us -> 63.8 us (0.954)
  starting transfers between devices: 22.1 us -> 20.1 us
  Pallas kernels: 26.1 us -> 24.3 us
  waiting for transfers between devices: 14.5 us -> 16.1 us
  local copies, waits for them, and re-layouts: 2.08 us -> 1.25 us
    pallas_call x7, Pallas kernels: 26.1 us -> 24.3 us  [on_chip(): pl.pallas_call(kernel, in_specs=specs[:count], out_specs=specs[count:] if...]
    all_to_all x2, starting transfers between devices: 12.6 us -> 11.5 us  [exchange(): lax.all_to_all(value, ('dom', 'dir'), split_axis=0, concat_axis=0, tiled=...]
    all_to_all x2, waiting for transfers between devices: 11.3 us -> 12.2 us  [exchange(): lax.all_to_all(value, ('dom', 'dir'), split_axis=0, concat_axis=0, tiled=...]
    ppermute x4, starting transfers between devices: 9.5 us -> 8.56 us  [both_ways(): return (lax.ppermute(value, axis, up), lax.ppermute(value, axis, down))]
    unnamed x15, local copies, waits for them, and re-layouts: 1.95 us -> 1.11 us
where the time goes in v2:
time: 63.8 us; the launch traced here: 63.4 us
  Pallas kernels  24.3 us (38%)
  starting transfers between devices  20.1 us (32%)
  waiting for transfers between devices  16.1 us (25%)
  other arithmetic  1.44 us (2%)
  local copies, waits for them, and re-layouts  1.25 us (2%)
    pallas_call x7, Pallas kernels, on_chip(): pl.pallas_call(kernel, in_specs=specs[:count], out_specs=specs[count:] if...  24.3 us
    all_to_all x2, waiting for transfers between devices, exchange(): lax.all_to_all(value, ('dom', 'dir'), split_axis=0, concat_axis=0, tiled=...  12.2 us
    all_to_all x2, starting transfers between devices, exchange(): lax.all_to_all(value, ('dom', 'dir'), split_axis=0, concat_axis=0, tiled=...  11.5 us
    ppermute x4, starting transfers between devices, both_ways(): return (lax.ppermute(value, axis, up), lax.ppermute(value, axis, down))  8.56 us
    ppermute x4, waiting for transfers between devices, both_ways(): return (lax.ppermute(value, axis, up), lax.ppermute(value, axis, down))  3.84 us
  transfers between devices with their start and end apart: 6, of which 3 were waited for; matrix products, arithmetic and copies ran while one was open for 4% of the time, Pallas kernels for 23%

profile of v2, /device:TPU:1, one launch (start us, length us, event | category | flops | bytes accessed | tf_op | source)
XLA Modules:
  0.0 63.4 jit_solution(14888443378621493676)
XLA Ops:
  0.0 2.5 %collective-permute-start = (bf16[4,8,1024]{2,1,0:T(8,128)(2,1)}, bf16[4,8,1024]{2,1,0:T(8,128)(2,1)}, u32[]{:S(2)}, u32[]{:S(2)}) collective-permute-start(bf16[4,8,1024]{2,1,0:T(8,128)(2,1)} %here_ref), channel_id=1, source_target_pairs={{0,8},{8,16},{16,24},{24,32},{32,40},{40,48},{48,56},{56,64},{64,7... | collective-permute-start | bytes 196616 | tf_op jit(solution)/shard_map/ppermute | solution.py:427
  2.5 4.6 %collective-permute-start.1 = (bf16[4,8,1024]{2,1,0:T(8,128)(2,1)}, bf16[4,8,1024]{2,1,0:T(8,128)(2,1)}, u32[]{:S(2)}, u32[]{:S(2)}) collective-permute-start(bf16[4,8,1024]{2,1,0:T(8,128)(2,1)} %here_ref), channel_id=1, source_target_pairs={{8,0},{16,8},{24,16},{32,24},{40,32},{48,40},{56,48},{64,56},{72,6... | collective-permute-start | bytes 196616 | tf_op jit(solution)/shard_map/ppermute | solution.py:427
  7.0 3.4 %shard_map.118 = (bf16[16,8,8,128]{3,2,1,0:T(8,128)(2,1)}, s32[8,128]{1,0:T(8,128)}) custom-call(bf16[4,8,1024]{2,1,0:T(8,128)(2,1)} %here_ref, s32[8,128]{1,0:T(8,128)} %bitcast.30), custom_call_target="tpu_custom_call" | custom-call | flops 8388608 | bytes 300000 | tf_op jit(solution)/shard_map/pallas_call | solution.py:36
  10.4 0.0 copy-start.5
  10.4 6.5 %all-to-all-start = ((bf16[128,8,128]{2,1,0:T(8,128)(2,1)}), bf16[128,8,128]{2,1,0:T(8,128)(2,1)S(1)}, u32[]{:S(2)}, u32[]{:S(2)}) async-start(bf16[128,8,128]{2,1,0:T(8,128)(2,1)} %bitcast.29), calls=%async_computation | async-start | bytes 524288 | tf_op jit(solution)/shard_map/all_to_all | solution.py:431
  16.9 0.7 %multiply_bitcast_fusion.kind_ref = s32[16,64]{1,0:T(8,128)S(1)} fusion(s32[64,16]{0,1:T(8,128)} %param.21), kind=kLoop, calls=%fused_computation.17 | loop fusion | flops 1024 | bytes 8192 | tf_op jit(solution)/shard_map/mul | solution.py:454
  17.6 0.7 %fusion.5.place_ref = s32[16,64]{1,0:T(8,128)S(1)} fusion(s32[64,16]{0,1:T(8,128)} %param.20, s32[]{:T(128)S(6)} %axis_index.23), kind=kLoop, calls=%fused_computation.13 | loop fusion | flops 35840 | bytes 8196 | tf_op jit(solution)/shard_map/mul | solution.py:453
  18.3 1.1 %copy.14 = f32[316,144]{1,0:T(8,128)S(1)} copy(f32[316,144]{0,1:T(8,128)} %param.19) | data formatting | bytes 364032
  19.5 0.0 collective-permute-done.before_ref
  19.5 0.0 collective-permute-done.1.after_ref
  19.5 8.4 %all-to-all-done.arrived_ref = bf16[128,8,128]{2,1,0:T(8,128)(2,1)S(1)} async-done(((bf16[128,8,128]{2,1,0:T(8,128)(2,1)}), bf16[128,8,128]{2,1,0:T(8,128)(2,1)S(1)}, u32[]{:S(2)}, u32[]{:S(2)}) %all-to-all-start) | async-done | bytes 262176 | tf_op jit(solution)/shard_map/all_to_all | solution.py:431
  27.9 0.0 copy-start
  27.9 4.1 %shard_map.119 = (bf16[72,8,128]{2,1,0:T(8,128)(2,1)S(1)}, bf16[64,8,256]{2,1,0:T(8,128)(2,1)S(1)}, bf16[64,144,256]{2,1,0:T(8,128)(2,1)S(1)}) custom-call(bf16[128,8,128]{2,1,0:T(8,128)(2,1)S(1)} %all-to-all-done.arrived_ref, bf16[64,144,256]{2,1,0:T(8,128)(2,1)} %bitcast.28), custom_call_target="tpu_custom_call" | custom-call | flops 37748736 | bytes 4718592 | tf_op jit(solution)/shard_map/pallas_call | solution.py:36
  32.0 1.4 %collective-permute-start.3 = (bf16[72,8,128]{2,1,0:T(8,128)(2,1)S(1)}, bf16[72,8,128]{2,1,0:T(8,128)(2,1)S(1)}, u32[]{:S(2)}, u32[]{:S(2)}) collective-permute-start(bf16[72,8,128]{2,1,0:T(8,128)(2,1)S(1)} %get-tuple-element.26.here_ref), channel_id=1, source_target_pairs={{8,0},{16,8},{24,16},{32,24},{40,32},{48,40},{56,48},{64,56},{72,6... | collective-permute-start | bytes 442376 | tf_op jit(solution)/shard_map/ppermute | solution.py:427
  33.4 0.2 collective-permute-start.2
  33.5 0.0 copy-done.5
  33.5 0.0 copy-done
  33.5 0.0 copy-start.6
  33.5 0.0 copy-start.1
  33.6 4.0 %shard_map.120.near_ref = f32[8,8,256]{2,1,0:T(8,128)S(1)} custom-call(s32[4,8]{1,0:T(4,128)S(1)} %bitcast.26, bf16[64,8,256]{2,1,0:T(8,128)(2,1)S(1)} %get-tuple-element.29.current_ref, bf16[8,4,256,256]{3,2,1,0:T(8,128)(2,1)S(1)} %copy-done), custom_call_target="tpu_custom_call" | custom-call | flops 33554432 | bytes 4194304 | tf_op jit(solution)/shard_map/pallas_call | solution.py:36
  37.6 0.0 collective-permute-done.3.after_ref
  37.6 3.8 %collective-permute-done.2.before_ref = bf16[72,8,128]{2,1,0:T(8,128)(2,1)S(1)} collective-permute-done((bf16[72,8,128]{2,1,0:T(8,128)(2,1)S(1)}, bf16[72,8,128]{2,1,0:T(8,128)(2,1)S(1)}, u32[]{:S(2)}, u32[]{:S(2)}) %collective-permute-start.2) | collective-permute-done | bytes 147488 | tf_op jit(solution)/shard_map/ppermute | solution.py:427
  41.4 4.9 %shard_map.121 = bf16[128,8,128]{2,1,0:T(8,128)(2,1)} custom-call(s32[16,64]{1,0:T(8,128)S(1)} %fusion.5.place_ref, s32[16,64]{1,0:T(8,128)S(1)} %multiply_bitcast_fusion.kind_ref, s32[1]{0:T(128)} %bitcast.4.own_ref, bf16[72,8,128]{2,1,0:T(8,128)(2,1)S(1)} %collective-permute-done.2.before_ref, bf16[72,8,128]{2,1,0:T(8,128)(2,1)S(1)} %get-tuple-element.26.here_ref, ...), custom_call_target="tpu_custom_call" | custom-call | flops 37748736 | bytes 4718592 | tf_op jit(solution)/shard_map/pallas_call | solution.py:36
  46.3 0.0 copy-start.2
  46.3 0.0 copy-start.3
  46.3 5.1 %all-to-all-start.1 = ((bf16[128,8,128]{2,1,0:T(8,128)(2,1)}), bf16[128,8,128]{2,1,0:T(8,128)(2,1)S(1)}, u32[]{:S(2)}, u32[]{:S(2)}) async-start(bf16[128,8,128]{2,1,0:T(8,128)(2,1)} %shard_map.121), calls=%async_computation.1 | async-start | bytes 524288 | tf_op jit(solution)/shard_map/all_to_all | solution.py:431
  51.3 0.0 copy-done.6
  51.4 0.0 copy-start.4
  51.4 0.1 reshape.22.source_ref
  51.5 0.0 copy-done.1
  51.5 4.4 %shard_map.122.schur_ref = f32[4,8,1024]{2,1,0:T(8,128)S(1)} custom-call(bf16[4,8,1024]{2,1,0:T(8,128)(2,1)S(1)} %copy-done.1, bf16[8,512,1024]{2,1,0:T(8,128)(2,1)} %bitcast.27), custom_call_target="tpu_custom_call" | custom-call | flops 67108864 | bytes 8388608 | tf_op jit(solution)/shard_map/pallas_call | solution.py:36
  55.9 0.0 copy-done.2
  55.9 0.0 copy-done.3
  55.9 2.8 %shard_map.123.base_ref = f32[4,8,1024]{2,1,0:T(8,128)S(1)} custom-call(s32[16]{0:T(128)S(1)} %reshape.22.source_ref, bf16[4,8,1024]{2,1,0:T(8,128)(2,1)} %collective-permute-done.before_ref, bf16[4,8,1024]{2,1,0:T(8,128)(2,1)S(1)} %copy-done.1, bf16[4,8,1024]{2,1,0:T(8,128)(2,1)} %collective-permute-done.1.after_ref, s32[4,4,1024]{2,1,0:T(4,128)S(1)} %copy-done.2, ...), custom_call_target="tpu_custom_call" | custom-call | flops 8388608 | bytes 8000000 | tf_op jit(solution)/shard_map/pallas_call | solution.py:36
  58.7 3.8 %all-to-all-done.1.term_ref = bf16[128,8,128]{2,1,0:T(8,128)(2,1)S(1)} async-done(((bf16[128,8,128]{2,1,0:T(8,128)(2,1)}), bf16[128,8,128]{2,1,0:T(8,128)(2,1)S(1)}, u32[]{:S(2)}, u32[]{:S(2)}) %all-to-all-start.1) | async-done | bytes 262176 | tf_op jit(solution)/shard_map/all_to_all | solution.py:431
  62.5 0.0 copy-done.4
  62.5 0.8 %shard_map.124 = f32[4,8,1024]{2,1,0:T(8,128)} custom-call(bf16[128,8,128]{2,1,0:T(8,128)(2,1)S(1)} %all-to-all-done.1.term_ref, s32[8,128]{1,0:T(8,128)S(1)} %copy-done.4, f32[4,8,1024]{2,1,0:T(8,128)S(1)} %shard_map.123.base_ref), custom_call_target="tpu_custom_call" | custom-call | flops 1048576 | bytes 600000 | tf_op jit(solution)/shard_map/pallas_call | solution.py:36
  (3 shorter events, 0.1 us)
Async XLA Ops:
  0.0 19.5 %collective-permute-start = (bf16[4,8,1024]{2,1,0:T(8,128)(2,1)}, bf16[4,8,1024]{2,1,0:T(8,128)(2,1)}, u32[]{:S(2)}, u32[]{:S(2)}) collective-permute-start(bf16[4,8,1024]{2,1,0:T(8,128)(2,1)} %here_ref), channel_id=1, source_target_pairs={{0,8},{8,16},{16,24},{24,32},{32,40},{40,48},{48,56},{56,64},{64,7... | collective-permute-start | bytes 196616 | tf_op jit(solution)/shard_map/ppermute | solution.py:427
  2.5 17.0 %collective-permute-start.1 = (bf16[4,8,1024]{2,1,0:T(8,128)(2,1)}, bf16[4,8,1024]{2,1,0:T(8,128)(2,1)}, u32[]{:S(2)}, u32[]{:S(2)}) collective-permute-start(bf16[4,8,1024]{2,1,0:T(8,128)(2,1)} %here_ref), channel_id=1, source_target_pairs={{8,0},{16,8},{24,16},{32,24},{40,32},{48,40},{56,48},{64,56},{72,6... | collective-permute-start | bytes 196616 | tf_op jit(solution)/shard_map/ppermute | solution.py:427
  10.4 23.1 %copy-start.5 = (s32[8,4]{0,1:T(4,128)S(1)}, s32[8,4]{0,1:T(4,128)}, u32[]{:S(2)}) copy-start(s32[8,4]{0,1:T(4,128)} %param.22) | copy-start | bytes 388
  10.4 17.5 %all-to-all-start = ((bf16[128,8,128]{2,1,0:T(8,128)(2,1)}), bf16[128,8,128]{2,1,0:T(8,128)(2,1)S(1)}, u32[]{:S(2)}, u32[]{:S(2)}) async-start(bf16[128,8,128]{2,1,0:T(8,128)(2,1)} %bitcast.29), calls=%async_computation | async-start | bytes 524288 | tf_op jit(solution)/shard_map/all_to_all | solution.py:431
  27.9 5.6 %copy-start = (bf16[8,4,256,256]{3,2,1,0:T(8,128)(2,1)S(1)}, bf16[8,4,256,256]{3,2,1,0:T(8,128)(2,1)}, u32[]{:S(2)}) copy-start(bf16[8,4,256,256]{3,2,1,0:T(8,128)(2,1)} %block_hbm.1) | copy-start | bytes 12582916
  32.0 5.6 %collective-permute-start.3 = (bf16[72,8,128]{2,1,0:T(8,128)(2,1)S(1)}, bf16[72,8,128]{2,1,0:T(8,128)(2,1)S(1)}, u32[]{:S(2)}, u32[]{:S(2)}) collective-permute-start(bf16[72,8,128]{2,1,0:T(8,128)(2,1)S(1)} %get-tuple-element.26.here_ref), channel_id=1, source_target_pairs={{8,0},{16,8},{24,16},{32,24},{40,32},{48,40},{56,48},{64,56},{72,6... | collective-permute-start | bytes 442376 | tf_op jit(solution)/shard_map/ppermute | solution.py:427
  33.4 8.1 %collective-permute-start.2 = (bf16[72,8,128]{2,1,0:T(8,128)(2,1)S(1)}, bf16[72,8,128]{2,1,0:T(8,128)(2,1)S(1)}, u32[]{:S(2)}, u32[]{:S(2)}) collective-permute-start(bf16[72,8,128]{2,1,0:T(8,128)(2,1)S(1)} %get-tuple-element.26.here_ref), channel_id=1, source_target_pairs={{0,8},{8,16},{16,24},{24,32},{32,40},{40,48},{48,56},{56,64},{64,7... | collective-permute-start | bytes 442376 | tf_op jit(solution)/shard_map/ppermute | solution.py:427
  33.5 17.8 %copy-start.6 = (s32[4,4]{1,0:T(4,128)S(1)}, s32[4,4]{1,0:T(4,128)}, u32[]{:S(2)}) copy-start(s32[4,4]{1,0:T(4,128)} %param.14) | copy-start | bytes 196
  33.5 17.9 %copy-start.1 = (bf16[4,8,1024]{2,1,0:T(8,128)(2,1)S(1)}, bf16[4,8,1024]{2,1,0:T(8,128)(2,1)}, u32[]{:S(2)}) copy-start(bf16[4,8,1024]{2,1,0:T(8,128)(2,1)} %here_ref) | copy-start | bytes 196612
  46.3 9.6 %copy-start.2 = (s32[4,4,1024]{2,1,0:T(4,128)S(1)}, s32[4,4,1024]{2,1,0:T(4,128)}, u32[]{:S(2)}) copy-start(s32[4,4,1024]{2,1,0:T(4,128)} %map_ref.1) | copy-start | bytes 196612
  46.3 9.6 %copy-start.3 = (f32[4,4,1024]{2,1,0:T(4,128)S(1)}, f32[4,4,1024]{2,1,0:T(4,128)}, u32[]{:S(2)}) copy-start(f32[4,4,1024]{2,1,0:T(4,128)} %coupling_ref.1) | copy-start | bytes 196612
  46.3 16.2 %all-to-all-start.1 = ((bf16[128,8,128]{2,1,0:T(8,128)(2,1)}), bf16[128,8,128]{2,1,0:T(8,128)(2,1)S(1)}, u32[]{:S(2)}, u32[]{:S(2)}) async-start(bf16[128,8,128]{2,1,0:T(8,128)(2,1)} %shard_map.121), calls=%async_computation.1 | async-start | bytes 524288 | tf_op jit(solution)/shard_map/all_to_all | solution.py:431
  51.4 11.2 %copy-start.4 = (s32[8,128]{1,0:T(8,128)S(1)}, s32[8,128]{1,0:T(8,128)}, u32[]{:S(2)}) copy-start(s32[8,128]{1,0:T(8,128)} %get-tuple-element.33.spot_ref) | copy-start | bytes 12292
